TPU v7x, 128 devices: a whole 4x4x4 slice. The times are simulated.
128 devices in a mesh: blk: 32 (over y, x, z_lo), grp: 4 (over z_hi, core).
Axes of the slice: x: 4, y: 4, z: 4 (z_hi: 2, z_lo: 2; z = z_hi * 2 + z_lo), core: 2. Of those that a mesh axis runs over, the one named last changes fastest.
Arguments:
- queries: float32 [16384, 1024], P(('blk', 'grp')), may hold values from -48 to 48
- passages: float32 [16384, 1024], P(('blk', 'grp')), may hold values from -48 to 48
- hard_table: bfloat16 [98304, 1024], P(('blk', 'grp')), may hold values from -12 to 12
- hard_index: int32 [16384, 8], P(('blk', 'grp')), may hold values from 0 to 3071, as said below
Outputs:
- mean_loss: float32 [], replicated
- query_grad: float32 [16384, 1024], P(('blk', 'grp'))
- passage_grad: float32 [16384, 1024], P(('blk', 'grp'))
- table_grad: bfloat16 [98304, 1024], P(('blk', 'grp'))
Inputs may be any that keep to these rules, and one draw needn't show every extreme that they name: Owner o = hard_index // 768 is a batch group of the query's own loop shard. Among the 1024 entries of one device, the four owners are named exactly 384, 256, 256 and 128 times in some order, and the owner named 3 * 128 times is the same for all devices of one loop shard; entries may repeat.
All inputs are finite; a program needn't handle non-finite values.
Results may differ from a plain program's by a relative error of at most 0.0038.
Values may be sent and summed in bfloat16 or wider, within the bound.
No kernel may reach another device: no remote copies, remote signals or barrier semaphores. Data moves between devices by JAX's collectives and lax.ppermute only.
A program may use at most 64 MiB of HBM per device.

v0:
```python
import jax
import jax.numpy as jnp
from jax import lax
from jax.sharding import Mesh
from jax.sharding import PartitionSpec as P

STOPS = 4
GRP = ("grp_0", "grp_1")
BLK = ("blk_0", "blk_1", "blk_2")
BLK_GRP = ("blk_0", "blk_1", "blk_2", "grp_0", "grp_1")


score_scale = 0.015625


def split_up(value, dim, length):
    shape = value.shape
    blocks = value.reshape(*shape[:dim], length, shape[dim] // length, *shape[dim + 1 :])
    return jnp.moveaxis(blocks, dim, 0)


def laid_out(blocks, dim):
    shape = list(blocks.shape[1:])
    shape[dim] *= blocks.shape[0]
    return jnp.moveaxis(blocks, 0, dim).reshape(shape)


def moved_by_axis(blocks, axes, order):
    inside = blocks.shape[1:]
    result = blocks.reshape(*(lax.axis_size(a) for a in axes), *inside)
    for k in order:
        result = lax.all_to_all(result, axes[k], k, k, tiled=True)
    return result.reshape(-1, *inside)


def exchange_by_chip(value, groups, order, split_dim, concat_dim):
    length = lax.axis_size(groups[0]) * lax.axis_size(groups[1])
    blocks = split_up(value, split_dim, length)
    return laid_out(moved_by_axis(blocks, groups, order), concat_dim)


def passed_along(value, axis, by):
    length = lax.axis_size(axis)
    return lax.ppermute(value, axis, [(i, (i + by) % length) for i in range(length)])


def by_axis(value, axes):
    for axis in axes:
        value = lax.psum(value, axis)
    return value


def pair_scores(query_blk, passage_block):
    return (
        lax.dot_general(
            query_blk,
            passage_block,
            (((1,), (1,)), ((), ())),
            precision=lax.Precision.HIGHEST,
            preferred_element_type=jnp.float32,
        )
        * score_scale
    )


def weighted_rows(weight, passage_block):
    return jnp.dot(
        weight, passage_block, precision=lax.Precision.HIGHEST, preferred_element_type=jnp.float32
    )


def weighted_queries(weight, query_blk):
    return lax.dot_general(
        weight,
        query_blk,
        (((0,), (0,)), ((), ())),
        precision=lax.Precision.HIGHEST,
        preferred_element_type=jnp.float32,
    )


def local(queries, passages, hard_table, hard_index):
    row_count, feature_width = queries.shape
    group_count = lax.axis_size(GRP)
    table_rows = hard_table.shape[0]
    slot_count = hard_index.shape[1]
    capacity = 3 * row_count
    flat_index = hard_index.reshape(-1)
    owner_id = flat_index // table_rows
    row_within = flat_index % table_rows
    owner_hot = (owner_id[:, None] == jnp.arange(group_count, dtype=jnp.int32)[None, :]).astype(
        jnp.int32
    )
    before = jnp.cumsum(owner_hot, axis=0) - owner_hot
    slot_rank = jnp.sum(before * owner_hot, axis=1)
    slot_dest = owner_id * capacity + slot_rank
    request = jnp.zeros((group_count * capacity,), jnp.int32).at[slot_dest].set(row_within)
    request = request.reshape(group_count, capacity)
    asked = lax.all_to_all(request, GRP, split_axis=0, concat_axis=0, tiled=True)
    picked = jnp.take(hard_table, asked, axis=0)
    returned = exchange_by_chip(picked, ("grp_0", "grp_1"), (1, 0), 0, 0)
    hard_vecs = returned.reshape(group_count * capacity, feature_width)[slot_dest]
    hard_vecs = hard_vecs.reshape(row_count, slot_count, feature_width).astype(jnp.float32)
    hard_scores = (
        jnp.einsum("rd,rkd->rk", queries, hard_vecs, precision=lax.Precision.HIGHEST) * score_scale
    )
    positive = jnp.sum(queries * passages, axis=1) * score_scale
    run_max = jnp.max(hard_scores, axis=1)
    run_sum = jnp.sum(jnp.exp(hard_scores - run_max[:, None]), axis=1)
    passage_block = passages
    kept_blocks = []
    kept_scores = []
    for stop_index in range(STOPS):
        if stop_index > 0:
            passage_block = passed_along(passage_block, BLK, 1)
        block_scores = pair_scores(queries, passage_block)
        kept_blocks.append(passage_block)
        kept_scores.append(block_scores)
        new_max = jnp.maximum(run_max, jnp.max(block_scores, axis=1))
        run_sum = run_sum * jnp.exp(run_max - new_max) + jnp.sum(
            jnp.exp(block_scores - new_max[:, None]), axis=1
        )
        run_max = new_max
    lse = run_max + jnp.log(run_sum)
    device_count = lax.axis_size(BLK) * lax.axis_size(GRP)
    total_loss = by_axis(jnp.sum(lse - positive), BLK_GRP)
    mean_loss = total_loss / (row_count * device_count)
    hard_weight = jnp.exp(hard_scores - lse[:, None])
    query_accum = jnp.einsum("rk,rkd->rd", hard_weight, hard_vecs, precision=lax.Precision.HIGHEST)
    grad_accum = None
    for stop_index in range(STOPS - 1, -1, -1):
        weight = jnp.exp(kept_scores[stop_index] - lse[:, None])
        query_accum = query_accum + weighted_rows(weight, kept_blocks[stop_index])
        contrib = weighted_queries(weight, queries)
        if grad_accum is None:
            grad_accum = contrib
        else:
            grad_accum = passed_along(grad_accum, BLK, -1) + contrib
    query_grad = score_scale * (query_accum - passages)
    passage_grad = score_scale * grad_accum - score_scale * queries
    hard_term = (score_scale * hard_weight[:, :, None] * queries[:, None, :]).astype(jnp.bfloat16)
    outgoing = jnp.zeros((group_count * capacity, feature_width), jnp.bfloat16)
    outgoing = outgoing.at[slot_dest].set(hard_term.reshape(row_count * slot_count, feature_width))
    outgoing = outgoing.reshape(group_count, capacity, feature_width)
    incoming = lax.all_to_all(outgoing, GRP, split_axis=0, concat_axis=0, tiled=True)
    table_accum = jnp.zeros((table_rows, feature_width), jnp.float32)
    table_accum = table_accum.at[asked.reshape(-1)].add(
        incoming.reshape(group_count * capacity, feature_width).astype(jnp.float32)
    )
    return (mean_loss, query_grad, passage_grad, table_accum.astype(jnp.bfloat16))


def solution(mesh):
    finer = Mesh(mesh.devices.reshape(4, 4, 2, 2, 2), ("blk_0", "blk_1", "blk_2", "grp_0", "grp_1"))
    in_specs = (P(BLK_GRP, None), P(BLK_GRP, None), P(BLK_GRP, None), P(BLK_GRP, None))
    out_specs = (P(), P(BLK_GRP, None), P(BLK_GRP, None), P(BLK_GRP, None))
    return jax.shard_map(local, mesh=finer, in_specs=in_specs, out_specs=out_specs, check_vma=False)
```

profile of v0, /device:TPU:1, one launch (start us, length us, event | category | flops | bytes accessed | tf_op | source)
XLA Modules:
  0.0 252.8 jit_solution(11918236442395781460)
XLA Ops:
  2.9 1.1 reduce-window.6
  5.0 4.3 %scatter_custom_fusion = s32[1536]{0:T(1024)S(1)} fusion(s32[1024]{0:T(1024)S(1)} %bitcast.72, s32[1024]{0:T(1024)S(1)} %get-tuple-element.14, s32[]{:T(128)} %constant.22.clone.1), kind=kCustom, calls=%fused_computation.83 | custom fusion | bytes 6148 | tf_op jit(solution)/shard_map/scatter | solution.py:97
  10.0 6.6 %all-to-all-start = ((s32[4,1,384]{2,1,0:T(1,128)}), s32[4,1,384]{2,1,0:T(1,128)S(1)}, u32[]{:S(2)}, u32[]{:S(2)}) async-start(s32[4,1,384]{2,1,0:T(1,128)} %all_to_all.19), calls=%async_computation | async-start | bytes 12288 | tf_op jit(solution)/shard_map/all_to_all | solution.py:99
  17.3 3.9 %all-to-all-done = s32[4,1,384]{2,1,0:T(1,128)S(1)} async-done(((s32[4,1,384]{2,1,0:T(1,128)}), s32[4,1,384]{2,1,0:T(1,128)S(1)}, u32[]{:S(2)}, u32[]{:S(2)}) %all-to-all-start) | async-done | bytes 6176 | tf_op jit(solution)/shard_map/all_to_all | solution.py:99
  21.4 5.8 %gather_fusion = bf16[1536,1024]{1,0:T(8,128)(2,1)} fusion(bf16[768,1024]{1,0:T(8,128)(2,1)S(1)} %copy-done, s32[2048]{0:T(1024)S(1)} %pad_clamp_fusion), kind=kCustom, calls=%fused_computation | custom fusion | bytes 6297600 | tf_op jit(solution)/shard_map/jit(_take)/gather | solution.py:100
  27.2 2.1 copy_select_fusion
  29.3 6.6 %all_to_all.30 = bf16[2,2,1,384,1024]{4,3,0,2,1:T(8,128)(2,1)S(1)} all-to-all(bf16[2,2,1,384,1024]{4,3,0,2,1:T(8,128)(2,1)S(1)} %copy_select_fusion), channel_id=1, replica_groups=mesh['blk_0'=4,'blk_1'=4,'blk_2'=2,'grp_0'=2,'grp_1'=2] {'grp_1'}, dimensions={1} | all-to-all | bytes 6291456 | tf_op jit(solution)/shard_map/all_to_all | solution.py:32
  35.9 2.0 copy.24
  37.9 5.3 %all-to-all-start.2 = ((bf16[2,2,1,384,1024]{4,3,1,2,0:T(8,128)(2,1)}), bf16[2,2,1,384,1024]{4,3,1,2,0:T(8,128)(2,1)}, u32[]{:S(2)}, u32[]{:S(2)}) async-start(bf16[2,2,1,384,1024]{4,3,1,2,0:T(8,128)(2,1)} %copy.24), calls=%async_computation.2 | async-start | bytes 6291456 | tf_op jit(solution)/shard_map/all_to_all | solution.py:32
  44.7 43.7 %collective-permute-done.1 = f32[128,1024]{1,0:T(8,128)S(1)} collective-permute-done((f32[128,1024]{1,0:T(8,128)S(1)}, f32[128,1024]{1,0:T(8,128)S(1)}, u32[]{:S(2)}, u32[]{:S(2)}) %collective-permute-start.1) | collective-permute-done | bytes 524320 | tf_op jit(solution)/shard_map/ppermute | solution.py:44
  88.4 2.3 collective-permute-start.2
  92.0 14.8 %collective-permute-done.2 = f32[128,1024]{1,0:T(8,128)S(1)} collective-permute-done((f32[128,1024]{1,0:T(8,128)S(1)}, f32[128,1024]{1,0:T(8,128)S(1)}, u32[]{:S(2)}, u32[]{:S(2)}) %collective-permute-start.2) | collective-permute-done | bytes 524320 | tf_op jit(solution)/shard_map/ppermute | solution.py:44
  108.2 8.3 %gather_fusion.1 = bf16[1024,1024]{1,0:T(8,128)(2,1)} fusion(bf16[1536,1024]{1,0:T(8,128)(2,1)} %bitcast.5, s32[1024]{0:T(1024)S(1)} %broadcast_clamp_fusion), kind=kCustom, calls=%fused_computation.1 | custom fusion | bytes 4198400 | tf_op jit(solution)/shard_map/gather | solution.py:102
  116.5 5.5 %fusion.7 = f32[128,1,8]{2,1,0:T(1,128)S(1)} fusion(bf16[1024,1024]{1,0:T(8,128)(2,1)} %gather_fusion.1, f32[128,1024,1]{1,0,2:T(8,128)S(1)} %bitcast.64), kind=kOutput, calls=%fused_computation.13 | convolution fusion | flops 12582912 | bytes 2625536 | tf_op jit(solution)/shard_map/rd,rkd->rk/dot_general | solution.py:105
  123.1 6.9 %psum.35 = f32[]{:T(128)} all-reduce(f32[]{:T(128)} %get-tuple-element.6), channel_id=1, replica_groups=mesh['blk_0'=4,'blk_1'=4,'blk_2'=2,'grp_0'=2,'grp_1'=2] {'blk_0'}, use_global_device_ids=true, to_apply=%region_16.17 | all-reduce | flops 1 | bytes 8 | tf_op jit(solution)/shard_map/psum | solution.py:49
  129.9 7.0 %psum.36 = f32[]{:T(128)} all-reduce(f32[]{:T(128)} %psum.35), channel_id=1, replica_groups=mesh['blk_0'=4,'blk_1'=4,'blk_2'=2,'grp_0'=2,'grp_1'=2] {'blk_1'}, use_global_device_ids=true, to_apply=%region_17.18 | all-reduce | flops 1 | bytes 8 | tf_op jit(solution)/shard_map/psum | solution.py:49
  136.9 4.9 %psum.37 = f32[]{:T(128)} all-reduce(f32[]{:T(128)} %psum.36), channel_id=1, replica_groups=mesh['blk_0'=4,'blk_1'=4,'blk_2'=2,'grp_0'=2,'grp_1'=2] {'blk_2'}, use_global_device_ids=true, to_apply=%region_18.19 | all-reduce | flops 1 | bytes 8 | tf_op jit(solution)/shard_map/psum | solution.py:49
  141.8 1.4 fusion.19
  144.0 5.9 %psum.38 = f32[]{:T(128)} all-reduce(f32[]{:T(128)} %psum.37), channel_id=1, replica_groups=mesh['blk_0'=4,'blk_1'=4,'blk_2'=2,'grp_0'=2,'grp_1'=2] {'grp_0'}, use_global_device_ids=true, to_apply=%region_19.20 | all-reduce | flops 1 | bytes 8 | tf_op jit(solution)/shard_map/psum | solution.py:49
  149.9 1.6 collective-permute-start.3
  151.5 7.8 %scatter_custom_fusion.1 = bf16[1536,1024]{1,0:T(8,128)(2,1)} fusion(s32[1024]{0:T(1024)S(1)} %bitcast.74, f32[128,1024]{1,0:T(8,128)S(1)} %copy-done.1, f32[1024]{0:T(1024)S(1)} %mul.123, bf16[]{:T(256)} %constant.61.clone.1), kind=kCustom, calls=%fused_computation.10 | custom fusion | flops 2097152 | bytes 3674114 | tf_op jit(solution)/shard_map/scatter | solution.py:143
  159.4 12.2 %all-to-all-start.3 = ((bf16[4,384,1024]{2,1,0:T(8,128)(2,1)}), bf16[4,384,1024]{2,1,0:T(8,128)(2,1)}, u32[]{:S(2)}, u32[]{:S(2)}) async-start(bf16[4,384,1024]{2,1,0:T(8,128)(2,1)} %bitcast.65), calls=%async_computation.3 | async-start | bytes 6291456 | tf_op jit(solution)/shard_map/all_to_all | solution.py:145
  171.6 1.4 fusion.24
  173.0 3.1 %psum.39 = f32[]{:T(128)} all-reduce(f32[]{:T(128)} %psum.38), channel_id=1, replica_groups=mesh['blk_0'=4,'blk_1'=4,'blk_2'=2,'grp_0'=2,'grp_1'=2] {'grp_1'}, use_global_device_ids=true, to_apply=%region_20.21 | all-reduce | flops 1 | bytes 8 | tf_op jit(solution)/shard_map/psum | solution.py:49
  178.0 1.7 convolution_add_fusion
  179.7 1.8 collective-permute-start.4
  182.1 1.8 fusion.5
  183.9 34.5 %collective-permute-done.4 = f32[128,1024]{1,0:T(8,128)S(1)} collective-permute-done((f32[128,1024]{1,0:T(8,128)S(1)}, f32[128,1024]{1,0:T(8,128)S(1)}, u32[]{:S(2)}, u32[]{:S(2)}) %collective-permute-start.4) | collective-permute-done | bytes 524320 | tf_op jit(solution)/shard_map/ppermute | solution.py:44
  219.8 1.6 fusion.17
  221.4 10.4 %collective-permute-done.5 = f32[128,1024]{1,0:T(8,128)S(1)} collective-permute-done((f32[128,1024]{1,0:T(8,128)S(1)}, f32[128,1024]{1,0:T(8,128)S(1)}, u32[]{:S(2)}, u32[]{:S(2)}) %collective-permute-start.5) | collective-permute-done | bytes 524320 | tf_op jit(solution)/shard_map/ppermute | solution.py:44
  232.7 15.7 %scatter_custom_fusion.2 = f32[768,1024]{1,0:T(8,128)} fusion(s32[1536]{0:T(1024)S(1)} %fusion.37, bf16[1536,1024]{1,0:T(8,128)(2,1)} %bitcast.18, f32[]{:T(128)} %constant.59.clone.1), kind=kCustom, calls=%fused_computation.5 | custom fusion | flops 3145728 | bytes 6291460 | tf_op jit(solution)/shard_map/scatter-add | solution.py:147
  248.4 3.3 %convert_element_type.26 = bf16[768,1024]{1,0:T(8,128)(2,1)} convert(f32[768,1024]{1,0:T(8,128)} %scatter_custom_fusion.2) | non-fusion elementwise | flops 786432 | bytes 4718592 | tf_op jit(solution)/shard_map/convert_element_type | solution.py:150
  (77 shorter events, 14.7 us)
Async XLA Ops:
  0.6 20.7 %copy-start = (bf16[768,1024]{1,0:T(8,128)(2,1)S(1)}, bf16[768,1024]{1,0:T(8,128)(2,1)}, u32[]{:S(2)}) copy-start(bf16[768,1024]{1,0:T(8,128)(2,1)} %param.6) | copy-start | bytes 4718596
  10.0 11.2 %all-to-all-start = ((s32[4,1,384]{2,1,0:T(1,128)}), s32[4,1,384]{2,1,0:T(1,128)S(1)}, u32[]{:S(2)}, u32[]{:S(2)}) async-start(s32[4,1,384]{2,1,0:T(1,128)} %all_to_all.19), calls=%async_computation | async-start | bytes 12288 | tf_op jit(solution)/shard_map/all_to_all | solution.py:99
  16.6 26.7 %collective-permute-start = (f32[128,1024]{1,0:T(8,128)}, f32[128,1024]{1,0:T(8,128)S(1)}, u32[]{:S(2)}, u32[]{:S(2)}) collective-permute-start(f32[128,1024]{1,0:T(8,128)} %param.5), channel_id=1, source_target_pairs={{0,4},{4,8},{8,12},{12,16},{16,20},{20,24},{24,28},{28,32},{32,36}... | collective-permute-start | bytes 1572872 | tf_op jit(solution)/shard_map/ppermute | solution.py:44
  37.9 6.2 %copy-start.1 = (f32[128,1024]{1,0:T(8,128)S(1)}, f32[128,1024]{1,0:T(8,128)}, u32[]{:S(2)}) copy-start(f32[128,1024]{1,0:T(8,128)} %param.4) | copy-start | bytes 1572868
  37.9 6.2 %copy-start.3 = (f32[128,1024]{1,0:T(8,128)S(1)}, f32[128,1024]{1,0:T(8,128)}, u32[]{:S(2)}) copy-start(f32[128,1024]{1,0:T(8,128)} %param.5) | copy-start | bytes 1572868
  37.9 70.2 %all-to-all-start.2 = ((bf16[2,2,1,384,1024]{4,3,1,2,0:T(8,128)(2,1)}), bf16[2,2,1,384,1024]{4,3,1,2,0:T(8,128)(2,1)}, u32[]{:S(2)}, u32[]{:S(2)}) async-start(bf16[2,2,1,384,1024]{4,3,1,2,0:T(8,128)(2,1)} %copy.24), calls=%async_computation.2 | async-start | bytes 6291456 | tf_op jit(solution)/shard_map/all_to_all | solution.py:32
  43.3 45.1 %collective-permute-start.1 = (f32[128,1024]{1,0:T(8,128)S(1)}, f32[128,1024]{1,0:T(8,128)S(1)}, u32[]{:S(2)}, u32[]{:S(2)}) collective-permute-start(f32[128,1024]{1,0:T(8,128)S(1)} %collective-permute-done), channel_id=1, source_target_pairs={{0,4},{4,8},{8,12},{12,16},{16,20},{20,24},{24,28},{28,32},{32,36}... | collective-permute-start | bytes 1572872 | tf_op jit(solution)/shard_map/ppermute | solution.py:44
  88.4 3.0 %copy-start.4 = (f32[128,1024]{1,0:T(8,128)}, f32[128,1024]{1,0:T(8,128)S(1)}, u32[]{:S(2)}) copy-start(f32[128,1024]{1,0:T(8,128)S(1)} %collective-permute-done.1) | copy-start | bytes 1572868
  88.4 18.4 %collective-permute-start.2 = (f32[128,1024]{1,0:T(8,128)S(1)}, f32[128,1024]{1,0:T(8,128)S(1)}, u32[]{:S(2)}, u32[]{:S(2)}) collective-permute-start(f32[128,1024]{1,0:T(8,128)S(1)} %collective-permute-done.1), channel_id=1, source_target_pairs={{0,4},{4,8},{8,12},{12,16},{16,20},{20,24},{24,28},{28,32},{32,36}... | collective-permute-start | bytes 1572872 | tf_op jit(solution)/shard_map/ppermute | solution.py:44
  106.8 0.8 copy-start.6
  149.9 28.1 %collective-permute-start.3 = (f32[128,1024]{1,0:T(8,128)}, f32[128,1024]{1,0:T(8,128)}, u32[]{:S(2)}, u32[]{:S(2)}) collective-permute-start(f32[128,1024]{1,0:T(8,128)} %fusion.19), channel_id=1, source_target_pairs={{0,124},{4,0},{8,4},{12,8},{16,12},{20,16},{24,20},{28,24},{32,28}... | collective-permute-start | bytes 1572872 | tf_op jit(solution)/shard_map/ppermute | solution.py:44
  159.4 73.3 %all-to-all-start.3 = ((bf16[4,384,1024]{2,1,0:T(8,128)(2,1)}), bf16[4,384,1024]{2,1,0:T(8,128)(2,1)}, u32[]{:S(2)}, u32[]{:S(2)}) async-start(bf16[4,384,1024]{2,1,0:T(8,128)(2,1)} %bitcast.65), calls=%async_computation.3 | async-start | bytes 6291456 | tf_op jit(solution)/shard_map/all_to_all | solution.py:145
  171.6 10.5 %copy-start.9 = (f32[128,8]{1,0:T(8,128)S(1)}, f32[128,8]{1,0:T(8,128)}, u32[]{:S(2)}) copy-start(f32[128,8]{1,0:T(8,128)} %get-tuple-element.5) | copy-start | bytes 12292
  176.7 5.4 %copy-start.2 = (bf16[1024,1024]{1,0:T(8,128)(2,1)S(1)}, bf16[1024,1024]{1,0:T(8,128)(2,1)}, u32[]{:S(2)}) copy-start(bf16[1024,1024]{1,0:T(8,128)(2,1)} %gather_fusion.1) | copy-start | bytes 6291460
  177.9 41.2 %copy-start.5 = (f32[128,1024]{1,0:T(8,128)S(1)}, f32[128,1024]{1,0:T(8,128)}, u32[]{:S(2)}) copy-start(f32[128,1024]{1,0:T(8,128)} %copy-done.4) | copy-start | bytes 1572868
  179.6 40.1 %copy-start.7 = (f32[128,1024]{1,0:T(8,128)S(1)}, f32[128,1024]{1,0:T(8,128)}, u32[]{:S(2)}) copy-start(f32[128,1024]{1,0:T(8,128)} %copy-done.6) | copy-start | bytes 1572868
  179.7 40.1 %copy-start.8 = (f32[128,1024]{1,0:T(8,128)S(1)}, f32[128,1024]{1,0:T(8,128)}, u32[]{:S(2)}) copy-start(f32[128,1024]{1,0:T(8,128)} %fusion.24) | copy-start | bytes 1572868
  179.7 38.8 %collective-permute-start.4 = (f32[128,1024]{1,0:T(8,128)S(1)}, f32[128,1024]{1,0:T(8,128)S(1)}, u32[]{:S(2)}, u32[]{:S(2)}) collective-permute-start(f32[128,1024]{1,0:T(8,128)S(1)} %convolution_add_fusion), channel_id=1, source_target_pairs={{0,124},{4,0},{8,4},{12,8},{16,12},{20,16},{24,20},{28,24},{32,28}... | collective-permute-start | bytes 1572872 | tf_op jit(solution)/shard_map/ppermute | solution.py:44
  218.5 13.3 %collective-permute-start.5 = (f32[128,1024]{1,0:T(8,128)S(1)}, f32[128,1024]{1,0:T(8,128)S(1)}, u32[]{:S(2)}, u32[]{:S(2)}) collective-permute-start(f32[128,1024]{1,0:T(8,128)S(1)} %add.160), channel_id=1, source_target_pairs={{0,124},{4,0},{8,4},{12,8},{16,12},{20,16},{24,20},{28,24},{32,28}... | collective-permute-start | bytes 1572872 | tf_op jit(solution)/shard_map/ppermute | solution.py:44
where the time goes:
time: 253 us
  waiting for transfers between devices  107 us (42%)
  other arithmetic  34.9 us (14%)
  blocking collectives  34.3 us (14%)
  starting transfers between devices  32 us (13%)
  local copies, waits for them, and re-layouts  23.4 us (9%)
  matrix products  18.3 us (7%)
  between operations  2.71 us (1%)
    ppermute x6, waiting for transfers between devices, passed_along(): lax.ppermute(value, axis, [(i, (i + by) % length) for i in range(length)])  103 us
    psum x5, blocking collectives, by_axis(): value = lax.psum(value, axis)  27.7 us
    scatter-add x1, other arithmetic, local(): table_accum.at[asked.reshape(-1)]  15.7 us
    all_to_all x1, starting transfers between devices, local(): lax.all_to_all(outgoing, GRP, split_axis=0, concat_axis=0, tiled=True)  12.2 us
    gather x1, local copies, waits for them, and re-layouts, local(): returned.reshape(group_count * capacity, feature_width)[slot_dest]  8.33 us
    scatter x1, other arithmetic, local(): outgoing.at[slot_dest]  7.83 us
    ppermute x6, starting transfers between devices, passed_along(): lax.ppermute(value, axis, [(i, (i + by) % length) for i in range(length)])  7.78 us
    all_to_all x1, starting transfers between devices, local(): lax.all_to_all(request, GRP, split_axis=0, concat_axis=0, tiled=True)  6.64 us
  transfers between devices with their start and end apart: 9, of which 5 were waited for; matrix products, arithmetic and copies ran while one was open for 12% of the time, Pallas kernels for 0%

commit v1 on v0

v1 whole, which is shorter than its diff:
```python
import jax
import jax.numpy as jnp
from jax import lax
from jax.experimental import pallas as pl
from jax.experimental.pallas import tpu as pltpu
from jax.sharding import Mesh
from jax.sharding import PartitionSpec as P


GRP = ("grp_0", "grp_1")
BLK = ("blk_0", "blk_1", "blk_2")
BLK_GRP = ("blk_0", "blk_1", "blk_2", "grp_0", "grp_1")

score_scale = 0.015625
FLOOR = -1.0e30
TABLE_BLOCK = 256
F32 = jnp.float32
BF16 = jnp.bfloat16


def along_loop(value, by):
    length = lax.axis_size(BLK)
    return lax.ppermute(value, BLK, [(i, (i + by) % length) for i in range(length)])


def swapped(value, axis):
    return lax.ppermute(value, axis, [(0, 1), (1, 0)])


def crossed(value):
    return lax.ppermute(value, GRP, [(0, 3), (1, 2), (2, 1), (3, 0)])


def mm(a, b, ca, cb):
    return lax.dot_general(a, b, (((ca,), (cb,)), ((), ())), preferred_element_type=F32)


def split2(x):
    hi = x.astype(BF16)
    return hi, (x - hi.astype(F32)).astype(BF16)


def split3(x):
    hi = x.astype(BF16)
    rest = x - hi.astype(F32)
    mid = rest.astype(BF16)
    return hi, mid, (rest - mid.astype(F32)).astype(BF16)


def table_scores(wide, index_rows, base):
    width = wide.shape[1] // 3
    score = (wide[:, :width] + (wide[:, width : 2 * width] + wide[:, 2 * width :])) * score_scale
    row_id = lax.broadcasted_iota(jnp.int32, score.shape, 0) + base
    count = jnp.zeros(score.shape, F32)
    for k in range(index_rows.shape[0]):
        count = count + jnp.where(index_rows[k : k + 1, :] == row_id, 1.0, 0.0)
    return jnp.where(count > 0.0, score + jnp.log(jnp.maximum(count, 1.0)), FLOOR)


class Source:
    def __init__(self, ref, copy=None):
        self.ref, self.copy = ref, copy

    def get(self):
        if self.copy is not None:
            self.copy.wait()
            self.copy = None
        return self.ref[...]


class Sink:
    def __init__(self, target, ref, sem):
        self.target, self.ref, self.sem, self.copies = target, ref, sem, []

    def start(self, target, ref):
        copy = pltpu.make_async_copy(ref, target, self.sem.at[len(self.copies)])
        copy.start()
        self.copies.append(copy)

    def put(self, value):
        self.ref[...] = value.astype(self.ref.dtype)
        self.start(self.target, self.ref)

    def put_rows(self, start, size, value):
        block = pl.ds(start, size)
        self.ref[block, :] = value.astype(self.ref.dtype)
        self.start(self.target.at[block, :], self.ref.at[block, :])

    def wait(self):
        for copy in self.copies:
            copy.wait()


HBM = pl.BlockSpec(memory_space=pltpu.HBM)
SMEM = pl.BlockSpec(memory_space=pltpu.SMEM)
VMEM = pl.BlockSpec(memory_space=pltpu.VMEM)


class Held:
    def __init__(self, value):
        self.value = value
        self.shape, self.dtype = value.shape, value.dtype


def bare(value):
    return value.value if isinstance(value, Held) else value


def call(body, outs, *args, scalars=0, mib=24, number=False):
    count = len(args)
    held = [k for k in range(scalars, count) if isinstance(args[k], Held)]

    def kernel(*refs):
        sinks = refs[count : count + len(outs)]
        extra = refs[count + len(outs) : count + len(outs) + number]
        scratch = refs[count + len(outs) + number :]
        sink_vmem, held_vmem = scratch[: len(outs)], scratch[len(outs) : len(outs) + len(held)]
        sink_sem, held_sem = scratch[-2], scratch[-1]
        sources = {}
        for k, slot in enumerate(held):
            copy = pltpu.make_async_copy(refs[slot], held_vmem[k], held_sem.at[k])
            copy.start()
            sources[slot] = Source(held_vmem[k], copy)
        results = [
            Sink(sinks[k], sink_vmem[k], sink_sem.at[k])
            for k in range(len(outs))
        ]
        body(*refs[:scalars], *(sources.get(k) or Source(refs[k]) for k in range(scalars, count)), *results, *extra)
        for result in results:
            result.wait()

    specs = [SMEM if k < scalars else HBM if k in held else VMEM for k in range(count)]
    results = pl.pallas_call(
        kernel,
        out_shape=[pltpu.HBM(s, d) for s, d in outs] + [jax.ShapeDtypeStruct((1,), F32)] * number,
        in_specs=specs,
        out_specs=[HBM] * len(outs) + [SMEM] * number,
        scratch_shapes=[pltpu.VMEM(s, d) for s, d in outs]
        + [pltpu.VMEM(args[k].shape, args[k].dtype) for k in held]
        + [pltpu.SemaphoreType.DMA((len(outs), 8)), pltpu.SemaphoreType.DMA((max(1, len(held)),))],
        compiler_params=pltpu.CompilerParams(vmem_limit_bytes=mib * 1024 * 1024),
    )(*(pltpu.with_memory_space_constraint(x.value, pltpu.HBM) if isinstance(x, Held) else x for x in args))
    return [Held(x) for x in results[: len(outs)]] + list(results[len(outs) :])


def pair_scores(blocks, query_parts):
    rows, width = blocks.shape[0], query_parts[0].shape[0]
    parts = split3(blocks)
    wide = mm(jnp.concatenate(parts, axis=0), jnp.concatenate(query_parts[:2], axis=0), 1, 1)
    small = wide[2 * rows :, :width] + wide[rows : 2 * rows, width:] + mm(parts[0], query_parts[2], 1, 1)
    return (wide[:rows, :width] + (wide[:rows, width:] + wide[rows : 2 * rows, :width] + small)) * score_scale


def hard_kernel(base_ref, qa, ia, qb, ib, table, na, nb, made_a, made_b, stat_a, stat_b, stack, first=None):
    a_parts, b_parts = split3(qa.get()), split3(qb.get())
    width = a_parts[0].shape[0]
    stack.put(jnp.concatenate(a_parts[:2] + b_parts[:2], axis=0))
    if first is not None:
        first(a_parts)
    wide = mm(table.get(), jnp.concatenate(a_parts + b_parts, axis=0), 1, 1)
    weights = []
    for slot, (index, named, stat) in enumerate(((ia, na, stat_a), (ib, nb, stat_b))):
        value = table_scores(wide[:, 3 * slot * width : 3 * (slot + 1) * width], index.get(), base_ref[0])
        named.put(value)
        top = jnp.max(value, axis=0, keepdims=True)
        value = jnp.exp(value - top)
        total = jnp.sum(value, axis=0, keepdims=True)
        stat.put(
            jnp.concatenate([jnp.broadcast_to(top, (4, width)), jnp.broadcast_to(total, (4, width))], axis=0)
        )
        weights += split2(value)
    pair = mm(jnp.concatenate(weights, axis=1), table.get(), 0, 0)
    made_a.put(pair[:width] + pair[width : 2 * width])
    made_b.put(pair[2 * width : 3 * width] + pair[3 * width :])


def first_hard_kernel(base_ref, qa, ia, qb, ib, table, passage, na, nb, made_a, made_b, stat_a, stat_b, stack, score):
    def first(parts):
        score.put(pair_scores(passage.get(), parts))

    hard_kernel(base_ref, qa, ia, qb, ib, table, na, nb, made_a, made_b, stat_a, stat_b, stack, first)


def is_eye(rows):
    shape = (rows, rows)
    return lax.broadcasted_iota(jnp.int32, shape, 0) == lax.broadcasted_iota(jnp.int32, shape, 1)


def window_kernel(query, p1, p2, p3, s0, t0, t1, t2, t3, w0, w1, w2, w3, lse, news):
    parts = split3(query.get())
    rows = parts[0].shape[0]
    blocks = jnp.concatenate([p1.get(), p2.get(), p3.get()], axis=0)
    found = pair_scores(blocks, parts)
    scores = [s0.get(), found[:rows], found[rows : 2 * rows], found[2 * rows :]]
    positive = jnp.sum(jnp.where(is_eye(rows), scores[0], 0.0), axis=0, keepdims=True)
    stats = [stat.get() for stat in (t0, t1, t2, t3)]
    top = stats[0][0:1]
    for stat in stats[1:]:
        top = jnp.maximum(top, stat[0:1])
    for score in scores:
        top = jnp.maximum(top, jnp.max(score, axis=0, keepdims=True))
    total = jnp.zeros_like(top)
    for stat in stats:
        total = total + stat[4:5] * jnp.exp(stat[0:1] - top)
    for score in scores:
        total = total + jnp.sum(jnp.exp(score - top), axis=0, keepdims=True)
    result = top + jnp.log(total)
    odd = lax.broadcasted_iota(jnp.int32, news.ref.shape, 0) % 2 == 1
    news.put(jnp.where(odd, result - positive, result))
    lse.put(jnp.broadcast_to(result, (8, rows)))
    for out, score in zip((w1, w2, w3, w0), scores[1:] + scores[:1]):
        out.put(jnp.exp(score - result))


def query_grad_kernel(
    lse, w0, w1, w2, w3, p0, p1, p2, p3, t0, t1, t2, t3, m0, m1, m2, m3, out
):
    row = lse.get()[0:1, :]
    rows = row.shape[1]
    eye = is_eye(rows)
    hi, lo = split2(jnp.concatenate([w.get() for w in (w0, w1, w2, w3)], axis=0))
    block_hi, block_lo = split2(jnp.concatenate([p.get() for p in (p0, p1, p2, p3)], axis=0))
    wide = mm(jnp.concatenate([hi, lo], axis=1), block_hi, 0, 0)
    total = wide[:rows] + (wide[rows:] + mm(hi, block_lo, 0, 0))
    for stat, made in ((t0, m0), (t1, m1), (t2, m2), (t3, m3)):
        ratio = jnp.broadcast_to(jnp.exp(stat.get()[0:1, :] - row), (rows, rows))
        column = jnp.sum(jnp.where(eye, ratio, 0.0), axis=1, keepdims=True)
        total = total + column * made.get().astype(F32)
    out.put(score_scale * (total - p0.get()))


def passage_grad_kernel(q0, q1, q2, q3, w0, w1, w2, w3, out):
    rows = w0.ref.shape[0]
    hi, lo = split2(jnp.concatenate([w.get() for w in (w0, w1, w2, w3)], axis=1))
    own_hi, own_lo = split2(q0.get())
    wide = mm(jnp.concatenate([hi, lo], axis=0), jnp.concatenate([own_hi, q1.get(), q2.get(), q3.get()], axis=0), 1, 0)
    total = wide[:rows] + (wide[rows:] + mm(hi[:, :rows], own_lo, 1, 0))
    out.put(score_scale * total - score_scale * q0.get())


def table_grad_kernel(base_ref, news, n0, n1, n2, n3, s01, s23, out, loss_ref):
    own = base_ref[2]
    rows_here = news.ref[pl.ds(pl.multiple_of(base_ref[1], 8), 8), :]
    lses = []
    for flip in range(4):
        lse = jnp.zeros((1, rows_here.shape[1]), F32)
        for owner in range(4):
            lse = lse + jnp.where((own ^ flip) == owner, rows_here[2 * owner : 2 * owner + 1, :], 0.0)
        lses.append(lse)
    stacks = [s01.get(), s23.get()]
    listed = [n.get() for n in (n0, n1, n2, n3)]
    size = TABLE_BLOCK
    for start in range(0, listed[0].shape[0], size):
        parts = []
        for value, lse in zip(listed, lses):
            weight = jnp.exp(value[start : start + size] - lse).astype(BF16)
            parts += [weight, weight]
        total = mm(jnp.concatenate(parts[:4], axis=1), stacks[0], 1, 0)
        total = total + mm(jnp.concatenate(parts[4:], axis=1), stacks[1], 1, 0)
        out.put_rows(start, size, score_scale * total)
    odd = lax.broadcasted_iota(jnp.int32, news.ref.shape, 0) % 2 == 1
    count = news.ref.shape[0] // 2 * news.ref.shape[1]
    loss_ref[0] = jnp.sum(jnp.where(odd, news.get(), 0.0)) / count


def named(move, value, *args, **kwargs):
    return move(bare(value), *args, **kwargs)


def step(queries, passages, hard_table, hard_index):
    rows, width = queries.shape
    table_rows = hard_table.shape[0]
    device_count = lax.axis_size(BLK) * lax.axis_size(GRP)
    index = hard_index.T
    mine = lax.axis_index(GRP).astype(jnp.int32)
    here = lax.axis_index(BLK).astype(jnp.int32)
    base = jnp.stack([mine * table_rows, here * 8, mine])
    short = queries.astype(BF16)
    queries, passages, hard_table = Held(queries), Held(passages), Held(hard_table)
    listed = ((table_rows, rows), F32)
    tile = ((8, rows), F32)
    full = ((rows, width), F32)
    half = ((rows, width), BF16)
    square = ((rows, rows), F32)
    stacked = ((4 * rows, width), BF16)

    q_far = named(swapped, queries, "grp_0")
    i_far = named(swapped, index, "grp_0")
    p_one = named(along_loop, passages, 1)
    p_two = named(along_loop, passages, 2)
    q_near = named(swapped, queries, "grp_1")
    i_near = named(swapped, index, "grp_1")
    n0, n1, made_0, near_made, stat_0, near_stat, stack_01, s0 = call(
        first_hard_kernel, [listed, listed, full, half, tile, tile, stacked, square],
        base, queries, index, q_near, i_near, hard_table, passages, scalars=1,
    )
    b_two = named(along_loop, short, -2)
    q_diag = named(swapped, q_far, "grp_1")
    i_diag = named(swapped, i_far, "grp_1")
    p_three = named(along_loop, p_one, 2)
    n2, n3, far_made, diag_made, far_stat, diag_stat, stack_23 = call(
        hard_kernel, [listed, listed, half, half, tile, tile, stacked],
        base, q_far, i_far, q_diag, i_diag, hard_table, scalars=1,
    )
    stat_1 = named(swapped, near_stat, "grp_1")
    stat_2 = named(swapped, far_stat, "grp_0")
    stat_3 = named(crossed, diag_stat)
    made_1 = named(swapped, near_made, "grp_1")
    made_2 = named(swapped, far_made, "grp_0")
    made_3 = named(crossed, diag_made)
    b_one = named(along_loop, short, -1)
    b_three = named(along_loop, b_one, -2)

    w0, w1, w2, w3, lse, news = call(
        window_kernel, [square, square, square, square, tile, ((2 * device_count, rows), F32)],
        queries, p_one, p_two, p_three, s0, stat_0, stat_1, stat_2, stat_3,
    )
    all_news = lax.all_to_all(bare(news), BLK_GRP, 0, 0, tiled=True)
    v1 = named(along_loop, w1, -1)
    v2 = named(along_loop, w2, -2)
    v3 = named(along_loop, w3, -3)

    (query_grad,) = call(
        query_grad_kernel, [full],
        lse, w0, w1, w2, w3, passages, p_one, p_two, p_three,
        stat_0, stat_1, stat_2, stat_3, made_0, made_1, made_2, made_3,
    )
    (passage_grad,) = call(
        passage_grad_kernel, [full],
        queries, b_one, b_two, b_three, w0, v1, v2, v3,
    )
    table_grad, mean_loss = call(
        table_grad_kernel, [((table_rows, width), BF16)],
        base, all_news, n0, n1, n2, n3, stack_01, stack_23, scalars=1, number=True,
    )
    return (mean_loss.reshape(()), bare(query_grad), bare(passage_grad), bare(table_grad))


def solution(mesh):
    finer = Mesh(mesh.devices.reshape(4, 4, 2, 2, 2), ("blk_0", "blk_1", "blk_2", "grp_0", "grp_1"))
    in_specs = (P(BLK_GRP, None), P(BLK_GRP, None), P(BLK_GRP, None), P(BLK_GRP, None))
    out_specs = (P(), P(BLK_GRP, None), P(BLK_GRP, None), P(BLK_GRP, None))
    return jax.shard_map(step, mesh=finer, in_specs=in_specs, out_specs=out_specs, check_vma=False)
```

time: 253 us -> 118 us (0.47)
  waiting for transfers between devices: 107 us -> 32 us
  blocking collectives: 34.3 us -> 0 us
  other arithmetic: 34.9 us -> 1.85 us
  Pallas kernels: 0 us -> 30.8 us
  local copies, waits for them, and re-layouts: 23.4 us -> 0.69 us
  starting transfers between devices: 32 us -> 50.4 us
  matrix products: 18.3 us -> 0 us
    ppermute x6 -> x21, waiting for transfers between devices: 103 us -> 32 us  [the longest x10 15.8 us: swapped(): return lax.ppermute(value, axis, [(0, 1), (1, 0)])]
    ppermute x6 -> x21, starting transfers between devices: 7.78 us -> 42 us  [the longest x9 21.9 us: along_loop(): lax.ppermute(value, BLK, [(i, (i + by) % length) for i in range(length)])]
    pallas_call x0 -> x6, Pallas kernels: none -> 30.8 us  [call(): pl.pallas_call(kernel, out_shape=[pltpu.HBM(s, d) for s, d in outs] + [ja...]
    psum x5 -> x0, blocking collectives: 27.7 us -> none  [by_axis(): value = lax.psum(value, axis)]
    dot_general x14 -> x0, matrix products: 18.3 us -> none  [the longest x1 5.51 us: local(): jnp.einsum('rd,rkd->rk', queries, hard_vecs, precision=lax.Precision.HIGH...]
    all_to_all x3 -> x1, starting transfers between devices: 24.2 us -> 8.31 us  [step(): all_news = lax.all_to_all(bare(news), BLK_GRP, 0, 0, tiled=True)]
    scatter-add x1 -> x0, other arithmetic: 15.7 us -> none  [local(): table_accum.at[asked.reshape(-1)]]
    gather x2 -> x0, local copies, waits for them, and re-layouts: 14.2 us -> none  [the longest x1 8.33 us: local(): returned.reshape(group_count * capacity, feature_width)[slot_dest]]
  transfers between devices with their start and end apart: 9 -> 22, of which waited for: 5 -> 8; matrix products, arithmetic and copies ran while one was open for 12% -> 2% of each run, Pallas kernels for 0% -> 24%
where the time goes in v1:
time: 118 us; the launch traced here: 117 us
  starting transfers between devices  50.4 us (43%)
  waiting for transfers between devices  32 us (27%)
  Pallas kernels  30.8 us (26%)
  other arithmetic  1.85 us (2%)
    pallas_call x6, Pallas kernels, call(): pl.pallas_call(kernel, out_shape=[pltpu.HBM(s, d) for s, d in outs] + [ja...  30.8 us
    ppermute x9, starting transfers between devices, along_loop(): lax.ppermute(value, BLK, [(i, (i + by) % length) for i in range(length)])  21.9 us
    ppermute x10, starting transfers between devices, swapped(): return lax.ppermute(value, axis, [(0, 1), (1, 0)])  19.6 us
    ppermute x10, waiting for transfers between devices, swapped(): return lax.ppermute(value, axis, [(0, 1), (1, 0)])  15.8 us
    ppermute x9, waiting for transfers between devices, along_loop(): lax.ppermute(value, BLK, [(i, (i + by) % length) for i in range(length)])  15.6 us
    all_to_all x1, starting transfers between devices, step(): all_news = lax.all_to_all(bare(news), BLK_GRP, 0, 0, tiled=True)  8.31 us
  transfers between devices with their start and end apart: 22, of which 8 were waited for; matrix products, arithmetic and copies ran while one was open for 2% of the time, Pallas kernels for 24%

profile of v1, /device:TPU:1, one launch (start us, length us, event | category | flops | bytes accessed | tf_op | source)
XLA Modules:
  0.0 116.7 jit_solution(3089400049349232083)
XLA Ops:
  0.6 4.5 %collective-permute-start.6 = (f32[128,1024]{1,0:T(8,128)}, f32[128,1024]{1,0:T(8,128)S(1)}, u32[]{:S(2)}, u32[]{:S(2)}) collective-permute-start(f32[128,1024]{1,0:T(8,128)} %refs_0_.3), channel_id=1, source_target_pairs={{0,2},{2,0},{1,3},{3,1},{4,6},{6,4},{5,7},{7,5},{8,10},{10,8},{9,1... | collective-permute-start | bytes 1572872 | tf_op jit(solution)/shard_map/ppermute | solution.py:27
  5.1 0.7 collective-permute-start
  5.9 1.2 %collective-permute-start.3 = (f32[128,1024]{1,0:T(8,128)}, f32[128,1024]{1,0:T(8,128)S(1)}, u32[]{:S(2)}, u32[]{:S(2)}) collective-permute-start(f32[128,1024]{1,0:T(8,128)} %refs_0_.3), channel_id=1, source_target_pairs={{0,1},{1,0},{2,3},{3,2},{4,5},{5,4},{6,7},{7,6},{8,9},{9,8},{10,11... | collective-permute-start | bytes 1572872 | tf_op jit(solution)/shard_map/ppermute | solution.py:27
  7.1 9.9 %collective-permute-done.6.refs_1_ = f32[128,1024]{1,0:T(8,128)S(1)} collective-permute-done((f32[128,1024]{1,0:T(8,128)}, f32[128,1024]{1,0:T(8,128)S(1)}, u32[]{:S(2)}, u32[]{:S(2)}) %collective-permute-start.6) | collective-permute-done | bytes 524320 | tf_op jit(solution)/shard_map/ppermute | solution.py:27
  17.0 2.1 %collective-permute-start.8 = (f32[128,1024]{1,0:T(8,128)S(1)}, f32[128,1024]{1,0:T(8,128)S(1)}, u32[]{:S(2)}, u32[]{:S(2)}) collective-permute-start(f32[128,1024]{1,0:T(8,128)S(1)} %collective-permute-done.6.refs_1_), channel_id=1, source_target_pairs={{0,1},{1,0},{2,3},{3,2},{4,5},{5,4},{6,7},{7,6},{8,9},{9,8},{10,11... | collective-permute-start | bytes 1572872 | tf_op jit(solution)/shard_map/ppermute | solution.py:27
  19.1 1.2 %collective-permute-start.1 = (f32[128,1024]{1,0:T(8,128)}, f32[128,1024]{1,0:T(8,128)S(1)}, u32[]{:S(2)}, u32[]{:S(2)}) collective-permute-start(f32[128,1024]{1,0:T(8,128)} %refs_5_.5), channel_id=1, source_target_pairs={{0,8},{4,12},{8,16},{12,20},{16,24},{20,28},{24,32},{28,36},{32,40... | collective-permute-start | bytes 1572872 | tf_op jit(solution)/shard_map/ppermute | solution.py:23
  20.3 7.0 %collective-permute-done.refs_1_.refs_6_ = f32[128,1024]{1,0:T(8,128)S(1)} collective-permute-done((f32[128,1024]{1,0:T(8,128)}, f32[128,1024]{1,0:T(8,128)S(1)}, u32[]{:S(2)}, u32[]{:S(2)}) %collective-permute-start) | collective-permute-done | bytes 524320 | tf_op jit(solution)/shard_map/ppermute | solution.py:23
  27.3 1.2 %collective-permute-start.2 = (f32[128,1024]{1,0:T(8,128)S(1)}, f32[128,1024]{1,0:T(8,128)S(1)}, u32[]{:S(2)}, u32[]{:S(2)}) collective-permute-start(f32[128,1024]{1,0:T(8,128)S(1)} %collective-permute-done.refs_1_.refs_6_), channel_id=1, source_target_pairs={{0,8},{4,12},{8,16},{12,20},{16,24},{20,28},{24,32},{28,36},{32,40... | collective-permute-start | bytes 1572872 | tf_op jit(solution)/shard_map/ppermute | solution.py:23
  28.8 4.2 %collective-permute-done.7.refs_2_ = s32[8,128]{1,0:T(8,128)S(1)} collective-permute-done((s32[8,128]{1,0:T(8,128)}, s32[8,128]{1,0:T(8,128)S(1)}, u32[]{:S(2)}, u32[]{:S(2)}) %collective-permute-start.7) | collective-permute-done | bytes 4128 | tf_op jit(solution)/shard_map/ppermute | solution.py:27
  33.0 2.7 %collective-permute-start.4 = (s32[8,128]{1,0:T(8,128)}, s32[8,128]{1,0:T(8,128)S(1)}, u32[]{:S(2)}, u32[]{:S(2)}) collective-permute-start(s32[8,128]{1,0:T(8,128)} %bitcast.9), channel_id=1, source_target_pairs={{0,1},{1,0},{2,3},{3,2},{4,5},{5,4},{6,7},{7,6},{8,9},{9,8},{10,11... | collective-permute-start | bytes 12296 | tf_op jit(solution)/shard_map/ppermute | solution.py:27
  35.6 1.0 collective-permute-done.4.refs_4_
  37.0 1.8 %convert_element_type.3 = bf16[128,1024]{1,0:T(8,128)(2,1)} convert(f32[128,1024]{1,0:T(8,128)} %refs_0_.3) | non-fusion elementwise | flops 131072 | bytes 786432 | tf_op jit(solution)/shard_map/convert_element_type | solution.py:278
  38.8 6.4 %collective-permute-start.15 = (bf16[128,1024]{1,0:T(8,128)(2,1)}, bf16[128,1024]{1,0:T(8,128)(2,1)S(1)}, u32[]{:S(2)}, u32[]{:S(2)}) collective-permute-start(bf16[128,1024]{1,0:T(8,128)(2,1)} %convert_element_type.3), channel_id=1, source_target_pairs={{0,124},{4,0},{8,4},{12,8},{16,12},{20,16},{24,20},{28,24},{32,28}... | collective-permute-start | bytes 786440 | tf_op jit(solution)/shard_map/ppermute | solution.py:23
  45.2 5.8 %collective-permute-done.15.refs_1_ = bf16[128,1024]{1,0:T(8,128)(2,1)S(1)} collective-permute-done((bf16[128,1024]{1,0:T(8,128)(2,1)}, bf16[128,1024]{1,0:T(8,128)(2,1)S(1)}, u32[]{:S(2)}, u32[]{:S(2)}) %collective-permute-start.15) | collective-permute-done | bytes 262176 | tf_op jit(solution)/shard_map/ppermute | solution.py:23
  51.0 1.2 %collective-permute-start.16 = (bf16[128,1024]{1,0:T(8,128)(2,1)}, bf16[128,1024]{1,0:T(8,128)(2,1)}, u32[]{:S(2)}, u32[]{:S(2)}) collective-permute-start(bf16[128,1024]{1,0:T(8,128)(2,1)} %convert_element_type.3), channel_id=1, source_target_pairs={{0,120},{4,124},{8,0},{12,4},{16,8},{20,12},{24,16},{28,20},{32,24... | collective-permute-start | bytes 786440 | tf_op jit(solution)/shard_map/ppermute | solution.py:23
  52.2 0.7 collective-permute-start.17
  53.0 0.7 copy-done
  53.7 7.8 %shard_map.75 = (f32[768,128]{1,0:T(8,128)}, f32[768,128]{1,0:T(8,128)}, f32[128,1024]{1,0:T(8,128)}, bf16[128,1024]{1,0:T(8,128)(2,1)}, f32[8,128]{1,0:T(8,128)...) custom-call(s32[3]{0:T(128)S(1)} %pad_add_fusion.refs_0_, f32[128,1024]{1,0:T(8,128)} %refs_0_.3, ...), custom_call_target="tpu_custom_call" | custom-call | tf_op jit(solution)/shard_map/pallas_call | solution.py:133
  61.5 1.7 %collective-permute-start.5 = (f32[8,128]{1,0:T(8,128)}, f32[8,128]{1,0:T(8,128)S(1)}, u32[]{:S(2)}, u32[]{:S(2)}) collective-permute-start(f32[8,128]{1,0:T(8,128)} %get-tuple-element.29), channel_id=1, source_target_pairs={{0,1},{1,0},{2,3},{3,2},{4,5},{5,4},{6,7},{7,6},{8,9},{9,8},{10,11... | collective-permute-start | bytes 12296 | tf_op jit(solution)/shard_map/ppermute | solution.py:27
  63.1 7.0 %shard_map.76 = (f32[768,128]{1,0:T(8,128)}, f32[768,128]{1,0:T(8,128)}, bf16[128,1024]{1,0:T(8,128)(2,1)}, bf16[128,1024]{1,0:T(8,128)(2,1)}, f32[8,128]{1,0:T(...) custom-call(s32[3]{0:T(128)S(1)} %pad_add_fusion.refs_0_, f32[128,1024]{1,0:T(8,128)S(1)} %collective-permute-done.6.refs_1_, ...), custom_call_target="tpu_custom_call" | custom-call | tf_op jit(solution)/shard_map/pallas_call | solution.py:133
  70.2 3.4 %collective-permute-start.10 = (f32[8,128]{1,0:T(8,128)}, f32[8,128]{1,0:T(8,128)S(1)}, u32[]{:S(2)}, u32[]{:S(2)}) collective-permute-start(f32[8,128]{1,0:T(8,128)} %get-tuple-element.30), channel_id=1, source_target_pairs={{0,2},{2,0},{1,3},{3,1},{4,6},{6,4},{5,7},{7,5},{8,10},{10,8},{9,1... | collective-permute-start | bytes 12296 | tf_op jit(solution)/shard_map/ppermute | solution.py:27
  74.1 0.7 collective-permute-done.10.refs_7_.refs_11_
  74.8 3.0 %collective-permute-start.13 = (bf16[128,1024]{1,0:T(8,128)(2,1)}, bf16[128,1024]{1,0:T(8,128)(2,1)S(1)}, u32[]{:S(2)}, u32[]{:S(2)}) collective-permute-start(bf16[128,1024]{1,0:T(8,128)(2,1)} %get-tuple-element.47), channel_id=1, source_target_pairs={{0,2},{2,0},{1,3},{3,1},{4,6},{6,4},{5,7},{7,5},{8,10},{10,8},{9,1... | collective-permute-start | bytes 786440 | tf_op jit(solution)/shard_map/ppermute | solution.py:27
  78.8 3.4 %shard_map.77 = (f32[128,128]{1,0:T(8,128)}, f32[128,128]{1,0:T(8,128)}, f32[128,128]{1,0:T(8,128)}, f32[128,128]{1,0:T(8,128)}, f32[8,128]{1,0:T(8,128)}, /*index=5*/f32[256,128]{1,0:T(8,128)}) custom-call(f32[128,1024]{1,0:T(8,128)} %refs_0_.3, f32[128,1024]{1,0:T(8,128)S(1)} %collective-permute-done.refs_1_.refs_6_, ...), custom_call_target="tpu_custom_call" | custom-call | tf_op jit(solution)/shard_map/pallas_call | solution.py:133
  82.3 3.9 %collective-permute-start.18 = (f32[128,128]{1,0:T(8,128)}, f32[128,128]{1,0:T(8,128)S(1)}, u32[]{:S(2)}, u32[]{:S(2)}) collective-permute-start(f32[128,128]{1,0:T(8,128)} %get-tuple-element.42.refs_2_), channel_id=1, source_target_pairs={{0,124},{4,0},{8,4},{12,8},{16,12},{20,16},{24,20},{28,24},{32,28}... | collective-permute-start | bytes 196616 | tf_op jit(solution)/shard_map/ppermute | solution.py:23
  86.2 8.3 %all-to-all-start = ((f32[128,2,128]{2,1,0:T(2,128)}), f32[128,2,128]{2,1,0:T(2,128)S(1)}, u32[]{:S(2)}, u32[]{:S(2)}) async-start(f32[128,2,128]{2,1,0:T(2,128)} %bitcast.11), calls=%async_computation | async-start | bytes 262144 | tf_op jit(solution)/shard_map/all_to_all | solution.py:318
  94.5 4.9 %collective-permute-start.19 = (f32[128,128]{1,0:T(8,128)}, f32[128,128]{1,0:T(8,128)S(1)}, u32[]{:S(2)}, u32[]{:S(2)}) collective-permute-start(f32[128,128]{1,0:T(8,128)} %get-tuple-element.43.refs_3_), channel_id=1, source_target_pairs={{0,120},{4,124},{8,0},{12,4},{16,8},{20,12},{24,16},{28,20},{32,24... | collective-permute-start | bytes 196616 | tf_op jit(solution)/shard_map/ppermute | solution.py:23
  99.4 1.7 %collective-permute-start.20 = (f32[128,128]{1,0:T(8,128)}, f32[128,128]{1,0:T(8,128)S(1)}, u32[]{:S(2)}, u32[]{:S(2)}) collective-permute-start(f32[128,128]{1,0:T(8,128)} %get-tuple-element.44.refs_4_), channel_id=1, source_target_pairs={{0,116},{4,120},{8,124},{12,0},{16,4},{20,8},{24,12},{28,16},{32,2... | collective-permute-start | bytes 196616 | tf_op jit(solution)/shard_map/ppermute | solution.py:23
  101.1 2.8 %collective-permute-done.20.refs_7_ = f32[128,128]{1,0:T(8,128)S(1)} collective-permute-done((f32[128,128]{1,0:T(8,128)}, f32[128,128]{1,0:T(8,128)S(1)}, u32[]{:S(2)}, u32[]{:S(2)}) %collective-permute-start.20) | collective-permute-done | bytes 65568 | tf_op jit(solution)/shard_map/ppermute | solution.py:23
  103.9 3.5 %shard_map.80 = f32[128,1024]{1,0:T(8,128)} custom-call(f32[128,1024]{1,0:T(8,128)} %refs_0_.3, bf16[128,1024]{1,0:T(8,128)(2,1)S(1)} %collective-permute-done.15.refs_1_, bf16[128,1024]{1,0:T(8,128)(2,1)} %collective-permute-done.16.refs_2_, bf16[128,1024]{1,0:T(8,128)(2,1)} %collective-permute-done.17.refs_3_, ...), custom_call_target="tpu_custom_call" | custom-call | tf_op jit(solution)/shard_map/pallas_call | solution.py:133
  107.4 5.9 %shard_map.78 = (bf16[768,1024]{1,0:T(8,128)(2,1)}, f32[1]{0:T(128)}) custom-call(s32[3]{0:T(128)S(1)} %pad_add_fusion.refs_0_, f32[256,128]{1,0:T(8,128)S(1)} %bitcast.7, f32[768,128]{1,0:T(8,128)} %get-tuple-element.33.refs_2_, f32[768,128]{1,0:T(8,128)} %get-tuple-element.34.refs_3_, f32[768,128]{1,0:T(8,128)} %get-tuple-element.35.refs_4_, ...), custom_call_target="tpu_custom_call" | custom-call | tf_op jit(solution)/shard_map/pallas_call | solution.py:133
  113.4 3.2 %shard_map.79 = f32[128,1024]{1,0:T(8,128)} custom-call(f32[8,128]{1,0:T(8,128)} %get-tuple-element.40.refs_0_, f32[128,128]{1,0:T(8,128)} %get-tuple-element.41.refs_1_.refs_4_, f32[128,128]{1,0:T(8,128)} %get-tuple-element.42.refs_2_, f32[128,128]{1,0:T(8,128)} %get-tuple-element.43.refs_3_, f32[128,128]{1,0:T(8,128)} %get-tuple-element.44.refs_4_, ...), custom_call_target="tpu_custom_call" | custom-call | tf_op jit(solution)/shard_map/pallas_call | solution.py:133
  (24 shorter events, 2.3 us)
Async XLA Ops:
  0.6 16.3 %collective-permute-start.6 = (f32[128,1024]{1,0:T(8,128)}, f32[128,1024]{1,0:T(8,128)S(1)}, u32[]{:S(2)}, u32[]{:S(2)}) collective-permute-start(f32[128,1024]{1,0:T(8,128)} %refs_0_.3), channel_id=1, source_target_pairs={{0,2},{2,0},{1,3},{3,1},{4,6},{6,4},{5,7},{7,5},{8,10},{10,8},{9,1... | collective-permute-start | bytes 1572872 | tf_op jit(solution)/shard_map/ppermute | solution.py:27
  5.1 22.2 %collective-permute-start = (f32[128,1024]{1,0:T(8,128)}, f32[128,1024]{1,0:T(8,128)S(1)}, u32[]{:S(2)}, u32[]{:S(2)}) collective-permute-start(f32[128,1024]{1,0:T(8,128)} %refs_5_.5), channel_id=1, source_target_pairs={{0,4},{4,8},{8,12},{12,16},{16,20},{20,24},{24,28},{28,32},{32,36}... | collective-permute-start | bytes 1572872 | tf_op jit(solution)/shard_map/ppermute | solution.py:23
  5.9 46.4 %collective-permute-start.3 = (f32[128,1024]{1,0:T(8,128)}, f32[128,1024]{1,0:T(8,128)S(1)}, u32[]{:S(2)}, u32[]{:S(2)}) collective-permute-start(f32[128,1024]{1,0:T(8,128)} %refs_0_.3), channel_id=1, source_target_pairs={{0,1},{1,0},{2,3},{3,2},{4,5},{5,4},{6,7},{7,6},{8,9},{9,8},{10,11... | collective-permute-start | bytes 1572872 | tf_op jit(solution)/shard_map/ppermute | solution.py:27
  17.0 44.5 %collective-permute-start.8 = (f32[128,1024]{1,0:T(8,128)S(1)}, f32[128,1024]{1,0:T(8,128)S(1)}, u32[]{:S(2)}, u32[]{:S(2)}) collective-permute-start(f32[128,1024]{1,0:T(8,128)S(1)} %collective-permute-done.6.refs_1_), channel_id=1, source_target_pairs={{0,1},{1,0},{2,3},{3,2},{4,5},{5,4},{6,7},{7,6},{8,9},{9,8},{10,11... | collective-permute-start | bytes 1572872 | tf_op jit(solution)/shard_map/ppermute | solution.py:27
  19.1 51.1 %collective-permute-start.1 = (f32[128,1024]{1,0:T(8,128)}, f32[128,1024]{1,0:T(8,128)S(1)}, u32[]{:S(2)}, u32[]{:S(2)}) collective-permute-start(f32[128,1024]{1,0:T(8,128)} %refs_5_.5), channel_id=1, source_target_pairs={{0,8},{4,12},{8,16},{12,20},{16,24},{20,28},{24,32},{28,36},{32,40... | collective-permute-start | bytes 1572872 | tf_op jit(solution)/shard_map/ppermute | solution.py:23
  27.3 46.3 %collective-permute-start.2 = (f32[128,1024]{1,0:T(8,128)S(1)}, f32[128,1024]{1,0:T(8,128)S(1)}, u32[]{:S(2)}, u32[]{:S(2)}) collective-permute-start(f32[128,1024]{1,0:T(8,128)S(1)} %collective-permute-done.refs_1_.refs_6_), channel_id=1, source_target_pairs={{0,8},{4,12},{8,16},{12,20},{16,24},{20,28},{24,32},{28,36},{32,40... | collective-permute-start | bytes 1572872 | tf_op jit(solution)/shard_map/ppermute | solution.py:23
  28.5 4.5 %collective-permute-start.7 = (s32[8,128]{1,0:T(8,128)}, s32[8,128]{1,0:T(8,128)S(1)}, u32[]{:S(2)}, u32[]{:S(2)}) collective-permute-start(s32[8,128]{1,0:T(8,128)} %bitcast.8), channel_id=1, source_target_pairs={{0,2},{2,0},{1,3},{3,1},{4,6},{6,4},{5,7},{7,5},{8,10},{10,8},{9,1... | collective-permute-start | bytes 12296 | tf_op jit(solution)/shard_map/ppermute | solution.py:27
  33.0 3.7 %collective-permute-start.4 = (s32[8,128]{1,0:T(8,128)}, s32[8,128]{1,0:T(8,128)S(1)}, u32[]{:S(2)}, u32[]{:S(2)}) collective-permute-start(s32[8,128]{1,0:T(8,128)} %bitcast.9), channel_id=1, source_target_pairs={{0,1},{1,0},{2,3},{3,2},{4,5},{5,4},{6,7},{7,6},{8,9},{9,8},{10,11... | collective-permute-start | bytes 12296 | tf_op jit(solution)/shard_map/ppermute | solution.py:27
  36.7 2.1 %collective-permute-start.9 = (s32[8,128]{1,0:T(8,128)S(1)}, s32[8,128]{1,0:T(8,128)S(1)}, u32[]{:S(2)}, u32[]{:S(2)}) collective-permute-start(s32[8,128]{1,0:T(8,128)S(1)} %collective-permute-done.7.refs_2_), channel_id=1, source_target_pairs={{0,1},{1,0},{2,3},{3,2},{4,5},{5,4},{6,7},{7,6},{8,9},{9,8},{10,11... | collective-permute-start | bytes 12296 | tf_op jit(solution)/shard_map/ppermute | solution.py:27
  38.8 12.2 %collective-permute-start.15 = (bf16[128,1024]{1,0:T(8,128)(2,1)}, bf16[128,1024]{1,0:T(8,128)(2,1)S(1)}, u32[]{:S(2)}, u32[]{:S(2)}) collective-permute-start(bf16[128,1024]{1,0:T(8,128)(2,1)} %convert_element_type.3), channel_id=1, source_target_pairs={{0,124},{4,0},{8,4},{12,8},{16,12},{20,16},{24,20},{28,24},{32,28}... | collective-permute-start | bytes 786440 | tf_op jit(solution)/shard_map/ppermute | solution.py:23
  51.0 31.2 %collective-permute-start.16 = (bf16[128,1024]{1,0:T(8,128)(2,1)}, bf16[128,1024]{1,0:T(8,128)(2,1)}, u32[]{:S(2)}, u32[]{:S(2)}) collective-permute-start(bf16[128,1024]{1,0:T(8,128)(2,1)} %convert_element_type.3), channel_id=1, source_target_pairs={{0,120},{4,124},{8,0},{12,4},{16,8},{20,12},{24,16},{28,20},{32,24... | collective-permute-start | bytes 786440 | tf_op jit(solution)/shard_map/ppermute | solution.py:23
  52.2 42.3 %collective-permute-start.17 = (bf16[128,1024]{1,0:T(8,128)(2,1)S(1)}, bf16[128,1024]{1,0:T(8,128)(2,1)}, u32[]{:S(2)}, u32[]{:S(2)}) collective-permute-start(bf16[128,1024]{1,0:T(8,128)(2,1)S(1)} %collective-permute-done.15.refs_1_), channel_id=1, source_target_pairs={{0,120},{4,124},{8,0},{12,4},{16,8},{20,12},{24,16},{28,20},{32,24... | collective-permute-start | bytes 786440 | tf_op jit(solution)/shard_map/ppermute | solution.py:23
  53.0 0.7 copy-start
  61.5 12.1 %copy-start.1 = (bf16[128,1024]{1,0:T(8,128)(2,1)S(1)}, bf16[128,1024]{1,0:T(8,128)(2,1)}, u32[]{:S(2)}) copy-start(bf16[128,1024]{1,0:T(8,128)(2,1)} %get-tuple-element.46) | copy-start | bytes 786436
  61.5 12.1 %collective-permute-start.5 = (f32[8,128]{1,0:T(8,128)}, f32[8,128]{1,0:T(8,128)S(1)}, u32[]{:S(2)}, u32[]{:S(2)}) collective-permute-start(f32[8,128]{1,0:T(8,128)} %get-tuple-element.29), channel_id=1, source_target_pairs={{0,1},{1,0},{2,3},{3,2},{4,5},{5,4},{6,7},{7,6},{8,9},{9,8},{10,11... | collective-permute-start | bytes 12296 | tf_op jit(solution)/shard_map/ppermute | solution.py:27
  70.2 4.6 %collective-permute-start.10 = (f32[8,128]{1,0:T(8,128)}, f32[8,128]{1,0:T(8,128)S(1)}, u32[]{:S(2)}, u32[]{:S(2)}) collective-permute-start(f32[8,128]{1,0:T(8,128)} %get-tuple-element.30), channel_id=1, source_target_pairs={{0,2},{2,0},{1,3},{3,1},{4,6},{6,4},{5,7},{7,5},{8,10},{10,8},{9,1... | collective-permute-start | bytes 12296 | tf_op jit(solution)/shard_map/ppermute | solution.py:27
  73.6 4.7 %collective-permute-start.11 = (f32[8,128]{1,0:T(8,128)}, f32[8,128]{1,0:T(8,128)S(1)}, u32[]{:S(2)}, u32[]{:S(2)}) collective-permute-start(f32[8,128]{1,0:T(8,128)} %get-tuple-element.31), channel_id=1, source_target_pairs={{0,3},{1,2},{2,1},{3,0},{4,7},{5,6},{6,5},{7,4},{8,11},{9,10},{10,... | collective-permute-start | bytes 12296 | tf_op jit(solution)/shard_map/ppermute | solution.py:31
  73.6 39.7 %collective-permute-start.12 = (bf16[128,1024]{1,0:T(8,128)(2,1)S(1)}, bf16[128,1024]{1,0:T(8,128)(2,1)S(1)}, u32[]{:S(2)}, u32[]{:S(2)}) collective-permute-start(bf16[128,1024]{1,0:T(8,128)(2,1)S(1)} %copy-done.1), channel_id=1, source_target_pairs={{0,1},{1,0},{2,3},{3,2},{4,5},{5,4},{6,7},{7,6},{8,9},{9,8},{10,11... | collective-permute-start | bytes 786440 | tf_op jit(solution)/shard_map/ppermute | solution.py:27
  74.8 38.5 %collective-permute-start.13 = (bf16[128,1024]{1,0:T(8,128)(2,1)}, bf16[128,1024]{1,0:T(8,128)(2,1)S(1)}, u32[]{:S(2)}, u32[]{:S(2)}) collective-permute-start(bf16[128,1024]{1,0:T(8,128)(2,1)} %get-tuple-element.47), channel_id=1, source_target_pairs={{0,2},{2,0},{1,3},{3,1},{4,6},{6,4},{5,7},{7,5},{8,10},{10,8},{9,1... | collective-permute-start | bytes 786440 | tf_op jit(solution)/shard_map/ppermute | solution.py:27
  78.3 35.0 %collective-permute-start.14 = (bf16[128,1024]{1,0:T(8,128)(2,1)}, bf16[128,1024]{1,0:T(8,128)(2,1)S(1)}, u32[]{:S(2)}, u32[]{:S(2)}) collective-permute-start(bf16[128,1024]{1,0:T(8,128)(2,1)} %get-tuple-element.48), channel_id=1, source_target_pairs={{0,3},{1,2},{2,1},{3,0},{4,7},{5,6},{6,5},{7,4},{8,11},{9,10},{10,... | collective-permute-start | bytes 786440 | tf_op jit(solution)/shard_map/ppermute | solution.py:31
  82.3 17.1 %collective-permute-start.18 = (f32[128,128]{1,0:T(8,128)}, f32[128,128]{1,0:T(8,128)S(1)}, u32[]{:S(2)}, u32[]{:S(2)}) collective-permute-start(f32[128,128]{1,0:T(8,128)} %get-tuple-element.42.refs_2_), channel_id=1, source_target_pairs={{0,124},{4,0},{8,4},{12,8},{16,12},{20,16},{24,20},{28,24},{32,28}... | collective-permute-start | bytes 196616 | tf_op jit(solution)/shard_map/ppermute | solution.py:23
  86.2 21.2 %all-to-all-start = ((f32[128,2,128]{2,1,0:T(2,128)}), f32[128,2,128]{2,1,0:T(2,128)S(1)}, u32[]{:S(2)}, u32[]{:S(2)}) async-start(f32[128,2,128]{2,1,0:T(2,128)} %bitcast.11), calls=%async_computation | async-start | bytes 262144 | tf_op jit(solution)/shard_map/all_to_all | solution.py:318
  94.5 6.6 %collective-permute-start.19 = (f32[128,128]{1,0:T(8,128)}, f32[128,128]{1,0:T(8,128)S(1)}, u32[]{:S(2)}, u32[]{:S(2)}) collective-permute-start(f32[128,128]{1,0:T(8,128)} %get-tuple-element.43.refs_3_), channel_id=1, source_target_pairs={{0,120},{4,124},{8,0},{12,4},{16,8},{20,12},{24,16},{28,20},{32,24... | collective-permute-start | bytes 196616 | tf_op jit(solution)/shard_map/ppermute | solution.py:23
  99.4 4.5 %collective-permute-start.20 = (f32[128,128]{1,0:T(8,128)}, f32[128,128]{1,0:T(8,128)S(1)}, u32[]{:S(2)}, u32[]{:S(2)}) collective-permute-start(f32[128,128]{1,0:T(8,128)} %get-tuple-element.44.refs_4_), channel_id=1, source_target_pairs={{0,116},{4,120},{8,124},{12,0},{16,4},{20,8},{24,12},{28,16},{32,2... | collective-permute-start | bytes 196616 | tf_op jit(solution)/shard_map/ppermute | solution.py:23

commit v2 on v1

--- a/solution.py
+++ b/solution.py
@@ -66,6 +66,14 @@
             self.copy.wait()
             self.copy = None
         return self.ref[...]
+
+    @property
+    def shape(self):
+        return self.ref.shape
+
+    def rows(self, start, size):
+        self.get()
+        return self.ref[pl.ds(start, size), :]
 
 
 class Sink:
@@ -157,10 +165,17 @@
     stack.put(jnp.concatenate(a_parts[:2] + b_parts[:2], axis=0))
     if first is not None:
         first(a_parts)
-    wide = mm(table.get(), jnp.concatenate(a_parts + b_parts, axis=0), 1, 1)
+    stack_all = jnp.concatenate(a_parts + b_parts, axis=0)
+    rows_in = table.get()
+    found = ([], [])
+    for start in range(0, rows_in.shape[0], TABLE_BLOCK):
+        wide = mm(rows_in[start : start + TABLE_BLOCK], stack_all, 1, 1)
+        for slot, index in enumerate((ia, ib)):
+            part = wide[:, 3 * slot * width : 3 * (slot + 1) * width]
+            found[slot].append(table_scores(part, index.get(), base_ref[0] + start))
     weights = []
-    for slot, (index, named, stat) in enumerate(((ia, na, stat_a), (ib, nb, stat_b))):
-        value = table_scores(wide[:, 3 * slot * width : 3 * (slot + 1) * width], index.get(), base_ref[0])
+    for values, named, stat in zip(found, (na, nb), (stat_a, stat_b)):
+        value = jnp.concatenate(values, axis=0)
         named.put(value)
         top = jnp.max(value, axis=0, keepdims=True)
         value = jnp.exp(value - top)
@@ -238,7 +253,7 @@
     out.put(score_scale * total - score_scale * q0.get())
 
 
-def table_grad_kernel(base_ref, news, n0, n1, n2, n3, s01, s23, out, loss_ref):
+def table_grad_kernel(base_ref, news, n0, n1, s01, n2, n3, s23, out, loss_ref):
     own = base_ref[2]
     rows_here = news.ref[pl.ds(pl.multiple_of(base_ref[1], 8), 8), :]
     lses = []
@@ -247,17 +262,17 @@
         for owner in range(4):
             lse = lse + jnp.where((own ^ flip) == owner, rows_here[2 * owner : 2 * owner + 1, :], 0.0)
         lses.append(lse)
-    stacks = [s01.get(), s23.get()]
-    listed = [n.get() for n in (n0, n1, n2, n3)]
-    size = TABLE_BLOCK
-    for start in range(0, listed[0].shape[0], size):
-        parts = []
-        for value, lse in zip(listed, lses):
-            weight = jnp.exp(value[start : start + size] - lse).astype(BF16)
-            parts += [weight, weight]
-        total = mm(jnp.concatenate(parts[:4], axis=1), stacks[0], 1, 0)
-        total = total + mm(jnp.concatenate(parts[4:], axis=1), stacks[1], 1, 0)
-        out.put_rows(start, size, score_scale * total)
+    halves = (((n0, lses[0]), (n1, lses[1]), s01), ((n2, lses[2]), (n3, lses[3]), s23))
+    for start in range(0, n0.shape[0], TABLE_BLOCK):
+        total = None
+        for first, second, stack in halves:
+            parts = []
+            for listed, lse in (first, second):
+                weight = jnp.exp(listed.rows(start, TABLE_BLOCK) - lse).astype(BF16)
+                parts += [weight, weight]
+            piece = mm(jnp.concatenate(parts, axis=1), stack.get(), 1, 0)
+            total = piece if total is None else total + piece
+        out.put_rows(start, TABLE_BLOCK, score_scale * total)
     odd = lax.broadcasted_iota(jnp.int32, news.ref.shape, 0) % 2 == 1
     count = news.ref.shape[0] // 2 * news.ref.shape[1]
     loss_ref[0] = jnp.sum(jnp.where(odd, news.get(), 0.0)) / count
@@ -331,7 +346,7 @@
     )
     table_grad, mean_loss = call(
         table_grad_kernel, [((table_rows, width), BF16)],
-        base, all_news, n0, n1, n2, n3, stack_01, stack_23, scalars=1, number=True,
+        base, all_news, n0, n1, stack_01, n2, n3, stack_23, scalars=1, number=True,
     )
     return (mean_loss.reshape(()), bare(query_grad), bare(passage_grad), bare(table_grad))
 

time: 118 us -> 117 us (level)
  Pallas kernels: 30.8 us -> 29.1 us
    pallas_call x6, Pallas kernels: 30.8 us -> 29.1 us  [call(): pl.pallas_call(kernel, out_shape=[pltpu.HBM(s, d) for s, d in outs] + [ja...]
  transfers between devices with their start and end apart: 22 -> 22, of which waited for: 8 -> 8; matrix products, arithmetic and copies ran while one was open for 2% -> 2% of each run, Pallas kernels for 24% -> 23%
where the time goes in v2:
time: 117 us; the launch traced here: 115 us
  starting transfers between devices  50.4 us (43%)
  waiting for transfers between devices  32 us (27%)
  Pallas kernels  29.1 us (25%)
  other arithmetic  1.85 us (2%)
    pallas_call x6, Pallas kernels, call(): pl.pallas_call(kernel, out_shape=[pltpu.HBM(s, d) for s, d in outs] + [ja...  29.1 us
    ppermute x9, starting transfers between devices, along_loop(): lax.ppermute(value, BLK, [(i, (i + by) % length) for i in range(length)])  21.9 us
    ppermute x10, starting transfers between devices, swapped(): return lax.ppermute(value, axis, [(0, 1), (1, 0)])  19.6 us
    ppermute x10, waiting for transfers between devices, swapped(): return lax.ppermute(value, axis, [(0, 1), (1, 0)])  15.8 us
    ppermute x9, waiting for transfers between devices, along_loop(): lax.ppermute(value, BLK, [(i, (i + by) % length) for i in range(length)])  15.6 us
    all_to_all x1, starting transfers between devices, step(): all_news = lax.all_to_all(bare(news), BLK_GRP, 0, 0, tiled=True)  8.31 us
  transfers between devices with their start and end apart: 22, of which 8 were waited for; matrix products, arithmetic and copies ran while one was open for 2% of the time, Pallas kernels for 23%

profile of v2, /device:TPU:1, one launch (start us, length us, event | category | flops | bytes accessed | tf_op | source)
XLA Modules:
  0.0 115.0 jit_solution(13104075053024991650)
XLA Ops:
  0.6 4.5 %collective-permute-start.6 = (f32[128,1024]{1,0:T(8,128)}, f32[128,1024]{1,0:T(8,128)S(1)}, u32[]{:S(2)}, u32[]{:S(2)}) collective-permute-start(f32[128,1024]{1,0:T(8,128)} %refs_0_.3), channel_id=1, source_target_pairs={{0,2},{2,0},{1,3},{3,1},{4,6},{6,4},{5,7},{7,5},{8,10},{10,8},{9,1... | collective-permute-start | bytes 1572872 | tf_op jit(solution)/shard_map/ppermute | solution.py:27
  5.1 0.7 collective-permute-start
  5.9 1.2 %collective-permute-start.3 = (f32[128,1024]{1,0:T(8,128)}, f32[128,1024]{1,0:T(8,128)S(1)}, u32[]{:S(2)}, u32[]{:S(2)}) collective-permute-start(f32[128,1024]{1,0:T(8,128)} %refs_0_.3), channel_id=1, source_target_pairs={{0,1},{1,0},{2,3},{3,2},{4,5},{5,4},{6,7},{7,6},{8,9},{9,8},{10,11... | collective-permute-start | bytes 1572872 | tf_op jit(solution)/shard_map/ppermute | solution.py:27
  7.1 9.9 %collective-permute-done.6.refs_1_ = f32[128,1024]{1,0:T(8,128)S(1)} collective-permute-done((f32[128,1024]{1,0:T(8,128)}, f32[128,1024]{1,0:T(8,128)S(1)}, u32[]{:S(2)}, u32[]{:S(2)}) %collective-permute-start.6) | collective-permute-done | bytes 524320 | tf_op jit(solution)/shard_map/ppermute | solution.py:27
  17.0 2.1 %collective-permute-start.8 = (f32[128,1024]{1,0:T(8,128)S(1)}, f32[128,1024]{1,0:T(8,128)S(1)}, u32[]{:S(2)}, u32[]{:S(2)}) collective-permute-start(f32[128,1024]{1,0:T(8,128)S(1)} %collective-permute-done.6.refs_1_), channel_id=1, source_target_pairs={{0,1},{1,0},{2,3},{3,2},{4,5},{5,4},{6,7},{7,6},{8,9},{9,8},{10,11... | collective-permute-start | bytes 1572872 | tf_op jit(solution)/shard_map/ppermute | solution.py:27
  19.1 1.2 %collective-permute-start.1 = (f32[128,1024]{1,0:T(8,128)}, f32[128,1024]{1,0:T(8,128)S(1)}, u32[]{:S(2)}, u32[]{:S(2)}) collective-permute-start(f32[128,1024]{1,0:T(8,128)} %refs_5_.5), channel_id=1, source_target_pairs={{0,8},{4,12},{8,16},{12,20},{16,24},{20,28},{24,32},{28,36},{32,40... | collective-permute-start | bytes 1572872 | tf_op jit(solution)/shard_map/ppermute | solution.py:23
  20.3 7.0 %collective-permute-done.refs_1_.refs_6_ = f32[128,1024]{1,0:T(8,128)S(1)} collective-permute-done((f32[128,1024]{1,0:T(8,128)}, f32[128,1024]{1,0:T(8,128)S(1)}, u32[]{:S(2)}, u32[]{:S(2)}) %collective-permute-start) | collective-permute-done | bytes 524320 | tf_op jit(solution)/shard_map/ppermute | solution.py:23
  27.3 1.2 %collective-permute-start.2 = (f32[128,1024]{1,0:T(8,128)S(1)}, f32[128,1024]{1,0:T(8,128)S(1)}, u32[]{:S(2)}, u32[]{:S(2)}) collective-permute-start(f32[128,1024]{1,0:T(8,128)S(1)} %collective-permute-done.refs_1_.refs_6_), channel_id=1, source_target_pairs={{0,8},{4,12},{8,16},{12,20},{16,24},{20,28},{24,32},{28,36},{32,40... | collective-permute-start | bytes 1572872 | tf_op jit(solution)/shard_map/ppermute | solution.py:23
  28.8 4.2 %collective-permute-done.7.refs_2_ = s32[8,128]{1,0:T(8,128)S(1)} collective-permute-done((s32[8,128]{1,0:T(8,128)}, s32[8,128]{1,0:T(8,128)S(1)}, u32[]{:S(2)}, u32[]{:S(2)}) %collective-permute-start.7) | collective-permute-done | bytes 4128 | tf_op jit(solution)/shard_map/ppermute | solution.py:27
  33.0 2.7 %collective-permute-start.4 = (s32[8,128]{1,0:T(8,128)}, s32[8,128]{1,0:T(8,128)S(1)}, u32[]{:S(2)}, u32[]{:S(2)}) collective-permute-start(s32[8,128]{1,0:T(8,128)} %bitcast.9), channel_id=1, source_target_pairs={{0,1},{1,0},{2,3},{3,2},{4,5},{5,4},{6,7},{7,6},{8,9},{9,8},{10,11... | collective-permute-start | bytes 12296 | tf_op jit(solution)/shard_map/ppermute | solution.py:27
  35.6 1.0 collective-permute-done.4.refs_4_
  37.0 1.8 %convert_element_type.3 = bf16[128,1024]{1,0:T(8,128)(2,1)} convert(f32[128,1024]{1,0:T(8,128)} %refs_0_.3) | non-fusion elementwise | flops 131072 | bytes 786432 | tf_op jit(solution)/shard_map/convert_element_type | solution.py:293
  38.8 6.4 %collective-permute-start.15 = (bf16[128,1024]{1,0:T(8,128)(2,1)}, bf16[128,1024]{1,0:T(8,128)(2,1)S(1)}, u32[]{:S(2)}, u32[]{:S(2)}) collective-permute-start(bf16[128,1024]{1,0:T(8,128)(2,1)} %convert_element_type.3), channel_id=1, source_target_pairs={{0,124},{4,0},{8,4},{12,8},{16,12},{20,16},{24,20},{28,24},{32,28}... | collective-permute-start | bytes 786440 | tf_op jit(solution)/shard_map/ppermute | solution.py:23
  45.2 5.8 %collective-permute-done.15.refs_1_ = bf16[128,1024]{1,0:T(8,128)(2,1)S(1)} collective-permute-done((bf16[128,1024]{1,0:T(8,128)(2,1)}, bf16[128,1024]{1,0:T(8,128)(2,1)S(1)}, u32[]{:S(2)}, u32[]{:S(2)}) %collective-permute-start.15) | collective-permute-done | bytes 262176 | tf_op jit(solution)/shard_map/ppermute | solution.py:23
  51.0 1.2 %collective-permute-start.16 = (bf16[128,1024]{1,0:T(8,128)(2,1)}, bf16[128,1024]{1,0:T(8,128)(2,1)}, u32[]{:S(2)}, u32[]{:S(2)}) collective-permute-start(bf16[128,1024]{1,0:T(8,128)(2,1)} %convert_element_type.3), channel_id=1, source_target_pairs={{0,120},{4,124},{8,0},{12,4},{16,8},{20,12},{24,16},{28,20},{32,24... | collective-permute-start | bytes 786440 | tf_op jit(solution)/shard_map/ppermute | solution.py:23
  52.2 0.7 collective-permute-start.17
  53.0 0.7 copy-done
  53.7 6.9 %shard_map.75 = (f32[768,128]{1,0:T(8,128)}, f32[768,128]{1,0:T(8,128)}, f32[128,1024]{1,0:T(8,128)}, bf16[128,1024]{1,0:T(8,128)(2,1)}, f32[8,128]{1,0:T(8,128)...) custom-call(s32[3]{0:T(128)S(1)} %pad_add_fusion.refs_0_, f32[128,1024]{1,0:T(8,128)} %refs_0_.3, ...), custom_call_target="tpu_custom_call" | custom-call | tf_op jit(solution)/shard_map/pallas_call | solution.py:141
  60.6 1.7 %collective-permute-start.5 = (f32[8,128]{1,0:T(8,128)}, f32[8,128]{1,0:T(8,128)S(1)}, u32[]{:S(2)}, u32[]{:S(2)}) collective-permute-start(f32[8,128]{1,0:T(8,128)} %get-tuple-element.29), channel_id=1, source_target_pairs={{0,1},{1,0},{2,3},{3,2},{4,5},{5,4},{6,7},{7,6},{8,9},{9,8},{10,11... | collective-permute-start | bytes 12296 | tf_op jit(solution)/shard_map/ppermute | solution.py:27
  62.3 6.3 %shard_map.76 = (f32[768,128]{1,0:T(8,128)}, f32[768,128]{1,0:T(8,128)}, bf16[128,1024]{1,0:T(8,128)(2,1)}, bf16[128,1024]{1,0:T(8,128)(2,1)}, f32[8,128]{1,0:T(...) custom-call(s32[3]{0:T(128)S(1)} %pad_add_fusion.refs_0_, f32[128,1024]{1,0:T(8,128)S(1)} %collective-permute-done.6.refs_1_, ...), custom_call_target="tpu_custom_call" | custom-call | tf_op jit(solution)/shard_map/pallas_call | solution.py:141
  68.6 3.4 %collective-permute-start.10 = (f32[8,128]{1,0:T(8,128)}, f32[8,128]{1,0:T(8,128)S(1)}, u32[]{:S(2)}, u32[]{:S(2)}) collective-permute-start(f32[8,128]{1,0:T(8,128)} %get-tuple-element.30), channel_id=1, source_target_pairs={{0,2},{2,0},{1,3},{3,1},{4,6},{6,4},{5,7},{7,5},{8,10},{10,8},{9,1... | collective-permute-start | bytes 12296 | tf_op jit(solution)/shard_map/ppermute | solution.py:27
  72.5 0.7 collective-permute-done.10.refs_7_.refs_11_
  73.2 3.0 %collective-permute-start.13 = (bf16[128,1024]{1,0:T(8,128)(2,1)}, bf16[128,1024]{1,0:T(8,128)(2,1)S(1)}, u32[]{:S(2)}, u32[]{:S(2)}) collective-permute-start(bf16[128,1024]{1,0:T(8,128)(2,1)} %get-tuple-element.47), channel_id=1, source_target_pairs={{0,2},{2,0},{1,3},{3,1},{4,6},{6,4},{5,7},{7,5},{8,10},{10,8},{9,1... | collective-permute-start | bytes 786440 | tf_op jit(solution)/shard_map/ppermute | solution.py:27
  77.2 3.4 %shard_map.77 = (f32[128,128]{1,0:T(8,128)}, f32[128,128]{1,0:T(8,128)}, f32[128,128]{1,0:T(8,128)}, f32[128,128]{1,0:T(8,128)}, f32[8,128]{1,0:T(8,128)}, /*index=5*/f32[256,128]{1,0:T(8,128)}) custom-call(f32[128,1024]{1,0:T(8,128)} %refs_0_.3, f32[128,1024]{1,0:T(8,128)S(1)} %collective-permute-done.refs_1_.refs_6_, ...), custom_call_target="tpu_custom_call" | custom-call | tf_op jit(solution)/shard_map/pallas_call | solution.py:141
  80.7 3.9 %collective-permute-start.18 = (f32[128,128]{1,0:T(8,128)}, f32[128,128]{1,0:T(8,128)S(1)}, u32[]{:S(2)}, u32[]{:S(2)}) collective-permute-start(f32[128,128]{1,0:T(8,128)} %get-tuple-element.42.refs_2_), channel_id=1, source_target_pairs={{0,124},{4,0},{8,4},{12,8},{16,12},{20,16},{24,20},{28,24},{32,28}... | collective-permute-start | bytes 196616 | tf_op jit(solution)/shard_map/ppermute | solution.py:23
  84.6 8.3 %all-to-all-start = ((f32[128,2,128]{2,1,0:T(2,128)}), f32[128,2,128]{2,1,0:T(2,128)S(1)}, u32[]{:S(2)}, u32[]{:S(2)}) async-start(f32[128,2,128]{2,1,0:T(2,128)} %bitcast.11), calls=%async_computation | async-start | bytes 262144 | tf_op jit(solution)/shard_map/all_to_all | solution.py:333
  92.9 4.9 %collective-permute-start.19 = (f32[128,128]{1,0:T(8,128)}, f32[128,128]{1,0:T(8,128)S(1)}, u32[]{:S(2)}, u32[]{:S(2)}) collective-permute-start(f32[128,128]{1,0:T(8,128)} %get-tuple-element.43.refs_3_), channel_id=1, source_target_pairs={{0,120},{4,124},{8,0},{12,4},{16,8},{20,12},{24,16},{28,20},{32,24... | collective-permute-start | bytes 196616 | tf_op jit(solution)/shard_map/ppermute | solution.py:23
  97.8 1.7 %collective-permute-start.20 = (f32[128,128]{1,0:T(8,128)}, f32[128,128]{1,0:T(8,128)S(1)}, u32[]{:S(2)}, u32[]{:S(2)}) collective-permute-start(f32[128,128]{1,0:T(8,128)} %get-tuple-element.44.refs_4_), channel_id=1, source_target_pairs={{0,116},{4,120},{8,124},{12,0},{16,4},{20,8},{24,12},{28,16},{32,2... | collective-permute-start | bytes 196616 | tf_op jit(solution)/shard_map/ppermute | solution.py:23
  99.5 2.8 %collective-permute-done.20.refs_7_ = f32[128,128]{1,0:T(8,128)S(1)} collective-permute-done((f32[128,128]{1,0:T(8,128)}, f32[128,128]{1,0:T(8,128)S(1)}, u32[]{:S(2)}, u32[]{:S(2)}) %collective-permute-start.20) | collective-permute-done | bytes 65568 | tf_op jit(solution)/shard_map/ppermute | solution.py:23
  102.3 3.5 %shard_map.80 = f32[128,1024]{1,0:T(8,128)} custom-call(f32[128,1024]{1,0:T(8,128)} %refs_0_.3, bf16[128,1024]{1,0:T(8,128)(2,1)S(1)} %collective-permute-done.15.refs_1_, bf16[128,1024]{1,0:T(8,128)(2,1)} %collective-permute-done.16.refs_2_, bf16[128,1024]{1,0:T(8,128)(2,1)} %collective-permute-done.17.refs_3_, ...), custom_call_target="tpu_custom_call" | custom-call | tf_op jit(solution)/shard_map/pallas_call | solution.py:141
  105.8 5.8 %shard_map.78 = (bf16[768,1024]{1,0:T(8,128)(2,1)}, f32[1]{0:T(128)}) custom-call(s32[3]{0:T(128)S(1)} %pad_add_fusion.refs_0_, f32[256,128]{1,0:T(8,128)S(1)} %bitcast.7, f32[768,128]{1,0:T(8,128)} %get-tuple-element.33.refs_2_, f32[768,128]{1,0:T(8,128)} %get-tuple-element.34.refs_3_, bf16[512,1024]{1,0:T(8,128)(2,1)} %get-tuple-element.35.refs_4_, ...), custom_call_target="tpu_custom_call" | custom-call | tf_op jit(solution)/shard_map/pallas_call | solution.py:141
  111.6 3.2 %shard_map.79 = f32[128,1024]{1,0:T(8,128)} custom-call(f32[8,128]{1,0:T(8,128)} %get-tuple-element.40.refs_0_, f32[128,128]{1,0:T(8,128)} %get-tuple-element.41.refs_1_.refs_4_, f32[128,128]{1,0:T(8,128)} %get-tuple-element.42.refs_2_, f32[128,128]{1,0:T(8,128)} %get-tuple-element.43.refs_3_, f32[128,128]{1,0:T(8,128)} %get-tuple-element.44.refs_4_, ...), custom_call_target="tpu_custom_call" | custom-call | tf_op jit(solution)/shard_map/pallas_call | solution.py:141
  (24 shorter events, 2.3 us)
Async XLA Ops:
  0.6 16.3 %collective-permute-start.6 = (f32[128,1024]{1,0:T(8,128)}, f32[128,1024]{1,0:T(8,128)S(1)}, u32[]{:S(2)}, u32[]{:S(2)}) collective-permute-start(f32[128,1024]{1,0:T(8,128)} %refs_0_.3), channel_id=1, source_target_pairs={{0,2},{2,0},{1,3},{3,1},{4,6},{6,4},{5,7},{7,5},{8,10},{10,8},{9,1... | collective-permute-start | bytes 1572872 | tf_op jit(solution)/shard_map/ppermute | solution.py:27
  5.1 22.2 %collective-permute-start = (f32[128,1024]{1,0:T(8,128)}, f32[128,1024]{1,0:T(8,128)S(1)}, u32[]{:S(2)}, u32[]{:S(2)}) collective-permute-start(f32[128,1024]{1,0:T(8,128)} %refs_5_.5), channel_id=1, source_target_pairs={{0,4},{4,8},{8,12},{12,16},{16,20},{20,24},{24,28},{28,32},{32,36}... | collective-permute-start | bytes 1572872 | tf_op jit(solution)/shard_map/ppermute | solution.py:23
  5.9 46.4 %collective-permute-start.3 = (f32[128,1024]{1,0:T(8,128)}, f32[128,1024]{1,0:T(8,128)S(1)}, u32[]{:S(2)}, u32[]{:S(2)}) collective-permute-start(f32[128,1024]{1,0:T(8,128)} %refs_0_.3), channel_id=1, source_target_pairs={{0,1},{1,0},{2,3},{3,2},{4,5},{5,4},{6,7},{7,6},{8,9},{9,8},{10,11... | collective-permute-start | bytes 1572872 | tf_op jit(solution)/shard_map/ppermute | solution.py:27
  17.0 43.6 %collective-permute-start.8 = (f32[128,1024]{1,0:T(8,128)S(1)}, f32[128,1024]{1,0:T(8,128)S(1)}, u32[]{:S(2)}, u32[]{:S(2)}) collective-permute-start(f32[128,1024]{1,0:T(8,128)S(1)} %collective-permute-done.6.refs_1_), channel_id=1, source_target_pairs={{0,1},{1,0},{2,3},{3,2},{4,5},{5,4},{6,7},{7,6},{8,9},{9,8},{10,11... | collective-permute-start | bytes 1572872 | tf_op jit(solution)/shard_map/ppermute | solution.py:27
  19.1 49.5 %collective-permute-start.1 = (f32[128,1024]{1,0:T(8,128)}, f32[128,1024]{1,0:T(8,128)S(1)}, u32[]{:S(2)}, u32[]{:S(2)}) collective-permute-start(f32[128,1024]{1,0:T(8,128)} %refs_5_.5), channel_id=1, source_target_pairs={{0,8},{4,12},{8,16},{12,20},{16,24},{20,28},{24,32},{28,36},{32,40... | collective-permute-start | bytes 1572872 | tf_op jit(solution)/shard_map/ppermute | solution.py:23
  27.3 44.7 %collective-permute-start.2 = (f32[128,1024]{1,0:T(8,128)S(1)}, f32[128,1024]{1,0:T(8,128)S(1)}, u32[]{:S(2)}, u32[]{:S(2)}) collective-permute-start(f32[128,1024]{1,0:T(8,128)S(1)} %collective-permute-done.refs_1_.refs_6_), channel_id=1, source_target_pairs={{0,8},{4,12},{8,16},{12,20},{16,24},{20,28},{24,32},{28,36},{32,40... | collective-permute-start | bytes 1572872 | tf_op jit(solution)/shard_map/ppermute | solution.py:23
  28.5 4.5 %collective-permute-start.7 = (s32[8,128]{1,0:T(8,128)}, s32[8,128]{1,0:T(8,128)S(1)}, u32[]{:S(2)}, u32[]{:S(2)}) collective-permute-start(s32[8,128]{1,0:T(8,128)} %bitcast.8), channel_id=1, source_target_pairs={{0,2},{2,0},{1,3},{3,1},{4,6},{6,4},{5,7},{7,5},{8,10},{10,8},{9,1... | collective-permute-start | bytes 12296 | tf_op jit(solution)/shard_map/ppermute | solution.py:27
  33.0 3.7 %collective-permute-start.4 = (s32[8,128]{1,0:T(8,128)}, s32[8,128]{1,0:T(8,128)S(1)}, u32[]{:S(2)}, u32[]{:S(2)}) collective-permute-start(s32[8,128]{1,0:T(8,128)} %bitcast.9), channel_id=1, source_target_pairs={{0,1},{1,0},{2,3},{3,2},{4,5},{5,4},{6,7},{7,6},{8,9},{9,8},{10,11... | collective-permute-start | bytes 12296 | tf_op jit(solution)/shard_map/ppermute | solution.py:27
  36.7 2.1 %collective-permute-start.9 = (s32[8,128]{1,0:T(8,128)S(1)}, s32[8,128]{1,0:T(8,128)S(1)}, u32[]{:S(2)}, u32[]{:S(2)}) collective-permute-start(s32[8,128]{1,0:T(8,128)S(1)} %collective-permute-done.7.refs_2_), channel_id=1, source_target_pairs={{0,1},{1,0},{2,3},{3,2},{4,5},{5,4},{6,7},{7,6},{8,9},{9,8},{10,11... | collective-permute-start | bytes 12296 | tf_op jit(solution)/shard_map/ppermute | solution.py:27
  38.8 12.2 %collective-permute-start.15 = (bf16[128,1024]{1,0:T(8,128)(2,1)}, bf16[128,1024]{1,0:T(8,128)(2,1)S(1)}, u32[]{:S(2)}, u32[]{:S(2)}) collective-permute-start(bf16[128,1024]{1,0:T(8,128)(2,1)} %convert_element_type.3), channel_id=1, source_target_pairs={{0,124},{4,0},{8,4},{12,8},{16,12},{20,16},{24,20},{28,24},{32,28}... | collective-permute-start | bytes 786440 | tf_op jit(solution)/shard_map/ppermute | solution.py:23
  51.0 29.7 %collective-permute-start.16 = (bf16[128,1024]{1,0:T(8,128)(2,1)}, bf16[128,1024]{1,0:T(8,128)(2,1)}, u32[]{:S(2)}, u32[]{:S(2)}) collective-permute-start(bf16[128,1024]{1,0:T(8,128)(2,1)} %convert_element_type.3), channel_id=1, source_target_pairs={{0,120},{4,124},{8,0},{12,4},{16,8},{20,12},{24,16},{28,20},{32,24... | collective-permute-start | bytes 786440 | tf_op jit(solution)/shard_map/ppermute | solution.py:23
  52.2 40.7 %collective-permute-start.17 = (bf16[128,1024]{1,0:T(8,128)(2,1)S(1)}, bf16[128,1024]{1,0:T(8,128)(2,1)}, u32[]{:S(2)}, u32[]{:S(2)}) collective-permute-start(bf16[128,1024]{1,0:T(8,128)(2,1)S(1)} %collective-permute-done.15.refs_1_), channel_id=1, source_target_pairs={{0,120},{4,124},{8,0},{12,4},{16,8},{20,12},{24,16},{28,20},{32,24... | collective-permute-start | bytes 786440 | tf_op jit(solution)/shard_map/ppermute | solution.py:23
  53.0 0.7 copy-start
  60.6 11.4 %copy-start.1 = (bf16[128,1024]{1,0:T(8,128)(2,1)S(1)}, bf16[128,1024]{1,0:T(8,128)(2,1)}, u32[]{:S(2)}) copy-start(bf16[128,1024]{1,0:T(8,128)(2,1)} %get-tuple-element.46) | copy-start | bytes 786436
  60.6 11.4 %collective-permute-start.5 = (f32[8,128]{1,0:T(8,128)}, f32[8,128]{1,0:T(8,128)S(1)}, u32[]{:S(2)}, u32[]{:S(2)}) collective-permute-start(f32[8,128]{1,0:T(8,128)} %get-tuple-element.29), channel_id=1, source_target_pairs={{0,1},{1,0},{2,3},{3,2},{4,5},{5,4},{6,7},{7,6},{8,9},{9,8},{10,11... | collective-permute-start | bytes 12296 | tf_op jit(solution)/shard_map/ppermute | solution.py:27
  68.6 4.6 %collective-permute-start.10 = (f32[8,128]{1,0:T(8,128)}, f32[8,128]{1,0:T(8,128)S(1)}, u32[]{:S(2)}, u32[]{:S(2)}) collective-permute-start(f32[8,128]{1,0:T(8,128)} %get-tuple-element.30), channel_id=1, source_target_pairs={{0,2},{2,0},{1,3},{3,1},{4,6},{6,4},{5,7},{7,5},{8,10},{10,8},{9,1... | collective-permute-start | bytes 12296 | tf_op jit(solution)/shard_map/ppermute | solution.py:27
  72.0 4.7 %collective-permute-start.11 = (f32[8,128]{1,0:T(8,128)}, f32[8,128]{1,0:T(8,128)S(1)}, u32[]{:S(2)}, u32[]{:S(2)}) collective-permute-start(f32[8,128]{1,0:T(8,128)} %get-tuple-element.31), channel_id=1, source_target_pairs={{0,3},{1,2},{2,1},{3,0},{4,7},{5,6},{6,5},{7,4},{8,11},{9,10},{10,... | collective-permute-start | bytes 12296 | tf_op jit(solution)/shard_map/ppermute | solution.py:31
  72.0 39.6 %collective-permute-start.12 = (bf16[128,1024]{1,0:T(8,128)(2,1)S(1)}, bf16[128,1024]{1,0:T(8,128)(2,1)S(1)}, u32[]{:S(2)}, u32[]{:S(2)}) collective-permute-start(bf16[128,1024]{1,0:T(8,128)(2,1)S(1)} %copy-done.1), channel_id=1, source_target_pairs={{0,1},{1,0},{2,3},{3,2},{4,5},{5,4},{6,7},{7,6},{8,9},{9,8},{10,11... | collective-permute-start | bytes 786440 | tf_op jit(solution)/shard_map/ppermute | solution.py:27
  73.2 38.4 %collective-permute-start.13 = (bf16[128,1024]{1,0:T(8,128)(2,1)}, bf16[128,1024]{1,0:T(8,128)(2,1)S(1)}, u32[]{:S(2)}, u32[]{:S(2)}) collective-permute-start(bf16[128,1024]{1,0:T(8,128)(2,1)} %get-tuple-element.47), channel_id=1, source_target_pairs={{0,2},{2,0},{1,3},{3,1},{4,6},{6,4},{5,7},{7,5},{8,10},{10,8},{9,1... | collective-permute-start | bytes 786440 | tf_op jit(solution)/shard_map/ppermute | solution.py:27
  76.8 34.9 %collective-permute-start.14 = (bf16[128,1024]{1,0:T(8,128)(2,1)}, bf16[128,1024]{1,0:T(8,128)(2,1)S(1)}, u32[]{:S(2)}, u32[]{:S(2)}) collective-permute-start(bf16[128,1024]{1,0:T(8,128)(2,1)} %get-tuple-element.48), channel_id=1, source_target_pairs={{0,3},{1,2},{2,1},{3,0},{4,7},{5,6},{6,5},{7,4},{8,11},{9,10},{10,... | collective-permute-start | bytes 786440 | tf_op jit(solution)/shard_map/ppermute | solution.py:31
  80.7 17.1 %collective-permute-start.18 = (f32[128,128]{1,0:T(8,128)}, f32[128,128]{1,0:T(8,128)S(1)}, u32[]{:S(2)}, u32[]{:S(2)}) collective-permute-start(f32[128,128]{1,0:T(8,128)} %get-tuple-element.42.refs_2_), channel_id=1, source_target_pairs={{0,124},{4,0},{8,4},{12,8},{16,12},{20,16},{24,20},{28,24},{32,28}... | collective-permute-start | bytes 196616 | tf_op jit(solution)/shard_map/ppermute | solution.py:23
  84.6 21.2 %all-to-all-start = ((f32[128,2,128]{2,1,0:T(2,128)}), f32[128,2,128]{2,1,0:T(2,128)S(1)}, u32[]{:S(2)}, u32[]{:S(2)}) async-start(f32[128,2,128]{2,1,0:T(2,128)} %bitcast.11), calls=%async_computation | async-start | bytes 262144 | tf_op jit(solution)/shard_map/all_to_all | solution.py:333
  92.9 6.6 %collective-permute-start.19 = (f32[128,128]{1,0:T(8,128)}, f32[128,128]{1,0:T(8,128)S(1)}, u32[]{:S(2)}, u32[]{:S(2)}) collective-permute-start(f32[128,128]{1,0:T(8,128)} %get-tuple-element.43.refs_3_), channel_id=1, source_target_pairs={{0,120},{4,124},{8,0},{12,4},{16,8},{20,12},{24,16},{28,20},{32,24... | collective-permute-start | bytes 196616 | tf_op jit(solution)/shard_map/ppermute | solution.py:23
  97.8 4.5 %collective-permute-start.20 = (f32[128,128]{1,0:T(8,128)}, f32[128,128]{1,0:T(8,128)S(1)}, u32[]{:S(2)}, u32[]{:S(2)}) collective-permute-start(f32[128,128]{1,0:T(8,128)} %get-tuple-element.44.refs_4_), channel_id=1, source_target_pairs={{0,116},{4,120},{8,124},{12,0},{16,4},{20,8},{24,12},{28,16},{32,2... | collective-permute-start | bytes 196616 | tf_op jit(solution)/shard_map/ppermute | solution.py:23
